TPU v7x, 512 devices: a whole 4x4x16 slice. The times are simulated.
512 devices in a mesh: group: 4 (over x), shard: 128 (over y, z, core).
Axes of the slice: x: 4, y: 4, z: 16, core: 2. Of those that a mesh axis runs over, the one named last changes fastest.
Arguments:
- amplitudes: float32 [524288, 128], P(('group', 'shard')), may hold values from -6 to 6
- orbit_index: int32 [524288, 128], P(('group', 'shard')), may hold values from 0 to 5
- requests: int32 [512, 512, 2], P(('group', 'shard')), may hold values from 0 to 1024, as said below
- targets: int32 [512, 512, 2], P(('group', 'shard')), may hold values from 0 to 1023
Outputs:
- image: float32 [524288, 128], P(('group', 'shard'))
Inputs may be any that keep to these rules, and one draw needn't show every extreme that they name: `requests`: each value is an owner's local block number below 1024, or 1024 for an empty slot; in every list from one requester to one owner the used slots come first; every draw has owners whose lists from every requester are full (2 blocks).
All inputs are finite; a program needn't handle non-finite values.
Results may differ from a plain program's by a relative error of at most 0.0003.
Values sent between devices are 32-bit elements; how exact they have to be, the bound alone decides.
No kernel may reach another device: no remote copies, remote signals or barrier semaphores. Data moves between devices by JAX's collectives and lax.ppermute only.
A program may use at most 64 MiB of HBM per device.

v0:
```python
import jax
import jax.numpy as jnp
from jax import lax
from jax.sharding import PartitionSpec as P


def in_blocks(shard, dim, peers):
    before, after = (shard.shape[:dim], shard.shape[dim + 1 :])
    return jnp.moveaxis(shard.reshape(*before, peers, -1, *after), dim, 0)


def joined_along(blocks, dim):
    blocks = jnp.moveaxis(blocks, 0, dim)
    shape = blocks.shape
    return blocks.reshape(*shape[:dim], shape[dim] * shape[dim + 1], *shape[dim + 2 :])


def joined_exchange(shard, axis, axes, splits, concats):
    sizes = [lax.axis_size(a) for a in axes]
    blocks = in_blocks(shard, splits[0], sizes[0])
    blocks = jnp.moveaxis(in_blocks(blocks, splits[1] + 1, sizes[1]), 0, 1)
    inside = blocks.shape[2:]
    blocks = blocks.reshape(-1, *inside)
    blocks = lax.all_to_all(blocks, axis, split_axis=0, concat_axis=0, tiled=True)
    blocks = joined_along(blocks.reshape(*sizes, *inside), concats[0] + 1)
    return joined_along(blocks, concats[1])


def per_device(amplitudes, orbit_index, requests, targets):
    blocks = amplitudes.shape[0]
    columns = amplitudes.shape[1]
    groups = lax.axis_size("group")
    shards = lax.axis_size("shard")
    factor = jnp.sqrt(96.0 * jnp.exp2(-orbit_index.astype(jnp.float32)))
    weighted = amplitudes * factor
    padded = jnp.concatenate([weighted, jnp.zeros((1, columns), jnp.float32)], axis=0)
    wanted = requests.reshape(groups, shards, -1)
    places = targets.reshape(groups, shards, -1)
    own_rows = weighted[places]
    incoming = lax.all_to_all(
        lax.all_to_all(wanted, "group", split_axis=0, concat_axis=0, tiled=True),
        "shard",
        split_axis=1,
        concat_axis=1,
        tiled=True,
    )
    received = joined_exchange(own_rows, ("group", "shard"), ("group", "shard"), (0, 1), (0, 1))
    served = padded[incoming]
    arrived = joined_exchange(served, ("group", "shard"), ("group", "shard"), (0, 1), (0, 1))
    pulled = jax.ops.segment_sum(
        arrived.reshape(-1, columns), places.reshape(-1), num_segments=blocks
    )
    pushed = jax.ops.segment_sum(
        received.reshape(-1, columns), incoming.reshape(-1), num_segments=blocks + 1
    )
    return (pulled + pushed[:blocks]) / factor


def solution(mesh):
    return jax.shard_map(
        per_device,
        mesh=mesh,
        in_specs=(
            P(("group", "shard"), None),
            P(("group", "shard"), None),
            P(("group", "shard"), None, None),
            P(("group", "shard"), None, None),
        ),
        out_specs=P(("group", "shard"), None),
        check_vma=False,
    )
```

profile of v0, /device:TPU:1, one launch (start us, length us, event | category | flops | bytes accessed | tf_op | source)
XLA Modules:
  0.0 145.5 jit_solution(14756938666408346302)
XLA Ops:
  0.0 0.0 copy-start.1
  0.0 5.0 %all-to-all-start = ((s32[4,128,2]{1,2,0:T(2,128)}), s32[4,128,2]{1,2,0:T(2,128)S(1)}, u32[]{:S(2)}, u32[]{:S(2)}) async-start(s32[4,128,2]{1,2,0:T(2,128)} %bitcast.33), calls=%async_computation | async-start | bytes 8192 | tf_op jit(solution)/shard_map/all_to_all | solution.py:41
  5.0 0.0 copy-done.1
  5.0 0.1 copy.19
  5.1 1.4 fusion.1
  6.6 0.2 reshape.54
  6.8 2.3 %all-to-all-done = s32[4,128,2]{1,2,0:T(2,128)S(1)} async-done(((s32[4,128,2]{1,2,0:T(2,128)}), s32[4,128,2]{1,2,0:T(2,128)S(1)}, u32[]{:S(2)}, u32[]{:S(2)}) %all-to-all-start) | async-done | bytes 4128 | tf_op jit(solution)/shard_map/all_to_all | solution.py:41
  9.1 0.8 copy.10
  9.9 21.2 %all-to-all-start.1 = ((s32[4,128,2]{0,2,1:T(2,128)}), s32[4,128,2]{0,2,1:T(2,128)S(1)}, u32[]{:S(2)}, u32[]{:S(2)}) async-start(s32[4,128,2]{0,2,1:T(2,128)} %copy.10), calls=%async_computation.1 | async-start | bytes 262144 | tf_op jit(solution)/shard_map/all_to_all | solution.py:40
  31.1 4.0 %gather_fusion = f32[1024,128]{1,0:T(8,128)} fusion(f32[1024,128]{1,0:T(8,128)S(1)} %fusion.1, s32[1024]{0:T(1024)S(1)} %broadcast_clamp_fusion.1), kind=kCustom, calls=%fused_computation | custom fusion | bytes 1052672 | tf_op jit(solution)/shard_map/gather | solution.py:39
  35.1 13.3 %all-to-all-done.1 = s32[4,128,2]{0,2,1:T(2,128)S(1)} async-done(((s32[4,128,2]{0,2,1:T(2,128)}), s32[4,128,2]{0,2,1:T(2,128)S(1)}, u32[]{:S(2)}, u32[]{:S(2)}) %all-to-all-start.1) | async-done | bytes 4128 | tf_op jit(solution)/shard_map/all_to_all | solution.py:40
  48.5 10.0 %all-to-all-start.2 = ((f32[512,1,1,2,128]{4,3,2,1,0:T(2,128)}), f32[512,1,1,2,128]{4,3,2,1,0:T(2,128)S(1)}, u32[]{:S(2)}, u32[]{:S(2)}) async-start(f32[512,1,1,2,128]{4,3,2,1,0:T(2,128)} %bitcast.3), calls=%async_computation.2 | async-start | bytes 1048576 | tf_op jit(solution)/shard_map/all_to_all | solution.py:24
  58.6 0.1 compare_select_fusion.1
  58.6 1.0 copy.17
  59.7 0.2 reshape.62
  59.9 4.0 %gather_fusion.1 = f32[1024,128]{1,0:T(8,128)} fusion(f32[1025,128]{1,0:T(8,128)S(1)} %concatenate.3, s32[1024]{0:T(1024)S(1)} %broadcast_clamp_fusion), kind=kCustom, calls=%fused_computation.1 | custom fusion | bytes 1052672 | tf_op jit(solution)/shard_map/gather | solution.py:48
  63.9 30.4 %all-to-all-done.2 = f32[512,1,1,2,128]{4,3,2,1,0:T(2,128)S(1)} async-done(((f32[512,1,1,2,128]{4,3,2,1,0:T(2,128)}), f32[512,1,1,2,128]{4,3,2,1,0:T(2,128)S(1)}, u32[]{:S(2)}, u32[]{:S(2)}) %all-to-all-start.2) | async-done | bytes 524320 | tf_op jit(solution)/shard_map/all_to_all | solution.py:24
  94.3 8.4 %all-to-all-start.3 = ((f32[512,1,1,2,128]{4,3,2,1,0:T(2,128)}), f32[512,1,1,2,128]{4,3,2,1,0:T(2,128)S(1)}, u32[]{:S(2)}, u32[]{:S(2)}) async-start(f32[512,1,1,2,128]{4,3,2,1,0:T(2,128)} %bitcast.10), calls=%async_computation.3 | async-start | bytes 1048576 | tf_op jit(solution)/shard_map/all_to_all | solution.py:24
  102.7 0.2 reshape.78
  102.8 1.0 copy.11
  103.8 0.2 reshape.70
  104.0 6.1 %scatter_custom_fusion = f32[1025,128]{1,0:T(8,128)S(1)} fusion(s32[1024]{0:T(1024)S(1)} %reshape.70, f32[1024,128]{1,0:T(8,128)S(1)} %bitcast.32, f32[]{:T(128)} %constant.6.clone.1), kind=kCustom, calls=%fused_computation.9 | custom fusion | flops 131072 | bytes 524804 | tf_op jit(solution)/shard_map/scatter-add | solution.py:53
  110.2 28.0 %all-to-all-done.3 = f32[512,1,1,2,128]{4,3,2,1,0:T(2,128)S(1)} async-done(((f32[512,1,1,2,128]{4,3,2,1,0:T(2,128)}), f32[512,1,1,2,128]{4,3,2,1,0:T(2,128)S(1)}, u32[]{:S(2)}, u32[]{:S(2)}) %all-to-all-start.3) | async-done | bytes 524320 | tf_op jit(solution)/shard_map/all_to_all | solution.py:24
  138.2 0.0 copy-start
  138.2 6.2 %scatter_fusion = f32[1024,128]{1,0:T(8,128)S(1)} fusion(f32[1024,128]{1,0:T(8,128)S(1)} %slice.8, s32[1024]{0:T(1024)S(1)} %reshape.78, f32[1024,128]{1,0:T(8,128)S(1)} %bitcast.31), kind=kCustom, calls=%fused_computation.3 | custom fusion | flops 131072 | bytes 1576960 | tf_op jit(solution)/shard_map/scatter-add | solution.py:50
  144.4 0.0 copy-done
  144.4 1.0 fusion
  (5 shorter events, 0.1 us)
Async XLA Ops:
  0.0 5.0 %copy-start.1 = (s32[1,512,2]{1,2,0:T(2,128)S(1)}, s32[1,512,2]{1,2,0:T(2,128)}, u32[]{:S(2)}) copy-start(s32[1,512,2]{1,2,0:T(2,128)} %param.7) | copy-start | bytes 12292
  0.0 9.1 %all-to-all-start = ((s32[4,128,2]{1,2,0:T(2,128)}), s32[4,128,2]{1,2,0:T(2,128)S(1)}, u32[]{:S(2)}, u32[]{:S(2)}) async-start(s32[4,128,2]{1,2,0:T(2,128)} %bitcast.33), calls=%async_computation | async-start | bytes 8192 | tf_op jit(solution)/shard_map/all_to_all | solution.py:41
  9.9 38.6 %all-to-all-start.1 = ((s32[4,128,2]{0,2,1:T(2,128)}), s32[4,128,2]{0,2,1:T(2,128)S(1)}, u32[]{:S(2)}, u32[]{:S(2)}) async-start(s32[4,128,2]{0,2,1:T(2,128)} %copy.10), calls=%async_computation.1 | async-start | bytes 262144 | tf_op jit(solution)/shard_map/all_to_all | solution.py:40
  48.5 45.8 %all-to-all-start.2 = ((f32[512,1,1,2,128]{4,3,2,1,0:T(2,128)}), f32[512,1,1,2,128]{4,3,2,1,0:T(2,128)S(1)}, u32[]{:S(2)}, u32[]{:S(2)}) async-start(f32[512,1,1,2,128]{4,3,2,1,0:T(2,128)} %bitcast.3), calls=%async_computation.2 | async-start | bytes 1048576 | tf_op jit(solution)/shard_map/all_to_all | solution.py:24
  94.3 43.9 %all-to-all-start.3 = ((f32[512,1,1,2,128]{4,3,2,1,0:T(2,128)}), f32[512,1,1,2,128]{4,3,2,1,0:T(2,128)S(1)}, u32[]{:S(2)}, u32[]{:S(2)}) async-start(f32[512,1,1,2,128]{4,3,2,1,0:T(2,128)} %bitcast.10), calls=%async_computation.3 | async-start | bytes 1048576 | tf_op jit(solution)/shard_map/all_to_all | solution.py:24
  138.2 6.2 %copy-start = (s32[1024,128]{1,0:T(8,128)S(1)}, s32[1024,128]{1,0:T(8,128)}, u32[]{:S(2)}) copy-start(s32[1024,128]{1,0:T(8,128)} %param.5) | copy-start | bytes 1572868
where the time goes:
time: 146 us; the launch traced here: 145 us
  waiting for transfers between devices  74.1 us (51%)
  starting transfers between devices  44.5 us (30%)
  other arithmetic  14.9 us (10%)
  local copies, waits for them, and re-layouts  11.8 us (8%)
    all_to_all x2, waiting for transfers between devices, joined_exchange(): lax.all_to_all(blocks, axis, split_axis=0, concat_axis=0, tiled=True)  58.4 us
    all_to_all x1, starting transfers between devices, per_device(): lax.all_to_all(lax.all_to_all(wanted, 'group', split_axis=0, concat_axis=...  21.2 us
    all_to_all x2, starting transfers between devices, joined_exchange(): lax.all_to_all(blocks, axis, split_axis=0, concat_axis=0, tiled=True)  18.4 us
    all_to_all x1, waiting for transfers between devices, per_device(): lax.all_to_all(lax.all_to_all(wanted, 'group', split_axis=0, concat_axis=...  13.3 us
    scatter-add x1, other arithmetic, per_device(): jax.ops.segment_sum(arrived.reshape(-1, columns), places.reshape(-1), num...  6.23 us
    scatter-add x1, other arithmetic, per_device(): jax.ops.segment_sum(received.reshape(-1, columns), incoming.reshape(-1),...  6.12 us
    all_to_all x1, starting transfers between devices, per_device(): lax.all_to_all(wanted, 'group', split_axis=0, concat_axis=0, tiled=True)  4.97 us
    gather x1, local copies, waits for them, and re-layouts, per_device(): own_rows = weighted[places]  4.04 us
  transfers between devices with their start and end apart: 4, of which 4 were waited for; matrix products, arithmetic and copies ran while one was open for 13% of the time, Pallas kernels for 0%

commit v1 on v0

v1 whole, which is shorter than its diff:
```python
import jax
import jax.numpy as jnp
from jax import lax
from jax.experimental import pallas as pl
from jax.experimental.pallas import tpu as pltpu
from jax.sharding import Mesh
from jax.sharding import PartitionSpec as P

AXES = ("x", "y", "z", "c")
PEERS = ("z", "x", "y", "c")
PLANE = ("x", "y", "c")


def orbit_factor(orbit):
    return jnp.sqrt(96.0 * jnp.exp2(-orbit.astype(jnp.float32)))


def two_parts(values):
    high = values.astype(jnp.bfloat16)
    low = (values - high.astype(jnp.float32)).astype(jnp.bfloat16)
    return jnp.concatenate([high, low], axis=1)


def halves_added(product):
    columns = product.shape[1] // 2
    return product[:, :columns] + product[:, columns:]


def weigh_kernel(amplitudes_ref, orbit_ref, table_ref):
    table_ref[...] = two_parts(amplitudes_ref[...] * orbit_factor(orbit_ref[...]))


def weigh(amplitudes, orbit):
    blocks, columns = amplitudes.shape
    return pl.pallas_call(
        weigh_kernel,
        out_shape=jax.ShapeDtypeStruct((blocks, 2 * columns), jnp.bfloat16),
        cost_estimate=pl.CostEstimate(
            flops=blocks * columns * 8,
            bytes_accessed=blocks * columns * 12,
            transcendentals=blocks * columns,
        ),
        name="weigh",
    )(amplitudes, orbit)


def pick_kernel(index_ref, table_ref, rows_ref, chosen_ref):
    groups, lanes = index_ref.shape
    blocks = table_ref.shape[0]
    lane = lax.broadcasted_iota(jnp.int32, (lanes, lanes), 1)
    for group in range(groups):
        numbers = jnp.broadcast_to(index_ref[group : group + 1, :], (lanes, lanes)).T
        for start in range(0, blocks, lanes):
            hit = numbers == lane + start
            chosen_ref[group * lanes : (group + 1) * lanes, start : start + lanes] = (
                jnp.where(hit, 1.0, 0.0).astype(jnp.bfloat16)
            )
    product = jnp.dot(
        chosen_ref[...], table_ref[...], preferred_element_type=jnp.float32
    )
    rows_ref[...] = halves_added(product)


def pick(index, table):
    rows = index.size
    blocks, width = table.shape
    return pl.pallas_call(
        pick_kernel,
        out_shape=jax.ShapeDtypeStruct((rows, width // 2), jnp.float32),
        scratch_shapes=[pltpu.VMEM((rows, blocks), jnp.bfloat16)],
        cost_estimate=pl.CostEstimate(
            flops=2 * rows * blocks * width,
            bytes_accessed=rows * width * 2 + blocks * width * 2,
            transcendentals=0,
        ),
        name="pick",
    )(index, table)


def gather_up_kernel(index_ref, rows_ref, orbit_ref, out_ref, chosen_ref):
    groups, lanes = index_ref.shape
    blocks = out_ref.shape[0]
    block = lax.broadcasted_iota(jnp.int32, (blocks, lanes), 0)
    for group in range(groups):
        hit = block == index_ref[group : group + 1, :]
        chosen_ref[:, group * lanes : (group + 1) * lanes] = jnp.where(
            hit, 1.0, 0.0
        ).astype(jnp.bfloat16)
    product = jnp.dot(
        chosen_ref[...], two_parts(rows_ref[...]), preferred_element_type=jnp.float32
    )
    out_ref[...] = halves_added(product) / orbit_factor(orbit_ref[...])


def gather_up(index, rows, orbit):
    blocks, columns = orbit.shape
    count = rows.shape[0]
    return pl.pallas_call(
        gather_up_kernel,
        out_shape=jax.ShapeDtypeStruct((blocks, columns), jnp.float32),
        scratch_shapes=[pltpu.VMEM((blocks, count), jnp.bfloat16)],
        cost_estimate=pl.CostEstimate(
            flops=4 * count * blocks * columns,
            bytes_accessed=(count + 2 * blocks) * columns * 4,
            transcendentals=blocks * columns,
        ),
        name="gather_up",
    )(index, rows, orbit)


def per_device(amplitudes, orbit_index, requests, targets):
    columns = amplitudes.shape[1]
    nx, ny, nz, nc = (lax.axis_size(a) for a in AXES)
    plane = nx * ny * nc
    slots = requests.shape[-1]
    asked = requests.reshape(nx, ny, nz, nc, slots).transpose(0, 1, 3, 4, 2)
    asked = asked.reshape(plane, slots, nz)
    asked = lax.all_to_all(asked, PLANE, split_axis=0, concat_axis=0, tiled=True)
    asked = asked.transpose(2, 0, 1).reshape(nz, 1, plane * slots)
    asked = lax.all_to_all(asked, "z", split_axis=0, concat_axis=0, tiled=True)
    incoming = asked.reshape(nz, plane, slots)
    places = targets.reshape(nx, ny, nz, nc, slots).transpose(2, 0, 1, 3, 4)
    places = places.reshape(nz, plane, slots)
    table = weigh(amplitudes, orbit_index)
    outgoing_index = jnp.concatenate([places, incoming], axis=-1).reshape(-1, 128)
    landing_index = jnp.concatenate([incoming, places], axis=-1).reshape(-1, 128)
    outgoing = pick(outgoing_index, table)
    arrived = lax.all_to_all(
        outgoing.reshape(nz * plane, 2 * slots, columns),
        PEERS,
        split_axis=0,
        concat_axis=0,
        tiled=True,
    )
    return gather_up(landing_index, arrived.reshape(-1, columns), orbit_index)


def solution(mesh):
    groups, shards = mesh.devices.shape
    devices = mesh.devices.reshape(groups, 4, shards // 8, 2)
    split = P(AXES)
    return jax.shard_map(
        per_device,
        mesh=Mesh(devices, AXES),
        in_specs=(split, split, split, split),
        out_specs=split,
        check_vma=False,
    )
```

time: 146 us -> 122 us (0.84)
  starting transfers between devices: 44.5 us -> 23.8 us
  blocking collectives: 0 us -> 16.9 us
  other arithmetic: 14.9 us -> 0.06 us
  Pallas kernels: 0 us -> 10.2 us
  waiting for transfers between devices: 74.1 us -> 66.1 us
  local copies, waits for them, and re-layouts: 11.8 us -> 4.7 us
    all_to_all x4 -> x2, starting transfers between devices: 44.5 us -> 23.8 us  [the longest x1 13.8 us: per_device(): asked = lax.all_to_all(asked, 'z', split_axis=0, concat_axis=0, tiled=True)]
    all_to_all x0 -> x1, blocking collectives: none -> 16.9 us  [per_device(): lax.all_to_all(asked, PLANE, split_axis=0, concat_axis=0, tiled=True)]
    scatter-add x2 -> x0, other arithmetic: 12.4 us -> none  [the longest x1 6.23 us: per_device(): jax.ops.segment_sum(arrived.reshape(-1, columns), places.reshape(-1), num...]
    pallas_call x0 -> x3, Pallas kernels: none -> 10.2 us  [the longest x1 4.04 us: gather_up(): pl.pallas_call(gather_up_kernel, out_shape=jax.ShapeDtypeStruct((blocks,...]
    gather x2 -> x0, local copies, waits for them, and re-layouts: 8.06 us -> none  [the longest x1 4.04 us: per_device(): own_rows = weighted[places]]
    all_to_all x4 -> x2, waiting for transfers between devices: 74.1 us -> 66.1 us  [the longest x1 57.6 us: per_device(): lax.all_to_all(outgoing.reshape(nz * plane, 2 * slots, columns), PEERS, s...]
    reshape x1 -> x6, local copies, waits for them, and re-layouts: 0.14 us -> 3.14 us  [the longest x1 0.89 us: per_device(): asked = requests.reshape(nx, ny, nz, nc, slots).transpose(0, 1, 3, 4, 2)]
    all_to_all x2 -> x1, local copies, waits for them, and re-layouts: 1.82 us -> 0.08 us  [per_device(): asked = lax.all_to_all(asked, 'z', split_axis=0, concat_axis=0, tiled=True)]
  transfers between devices with their start and end apart: 4 -> 2, of which waited for: 4 -> 2; matrix products, arithmetic and copies ran while one was open for 13% -> 1% of each run, Pallas kernels for 0% -> 2%
where the time goes in v1:
time: 122 us
  waiting for transfers between devices  66.1 us (54%)
  starting transfers between devices  23.8 us (20%)
  blocking collectives  16.9 us (14%)
  Pallas kernels  10.2 us (8%)
  local copies, waits for them, and re-layouts  4.7 us (4%)
    all_to_all x1, waiting for transfers between devices, per_device(): lax.all_to_all(outgoing.reshape(nz * plane, 2 * slots, columns), PEERS, s...  57.6 us
    all_to_all x1, blocking collectives, per_device(): lax.all_to_all(asked, PLANE, split_axis=0, concat_axis=0, tiled=True)  16.9 us
    all_to_all x1, starting transfers between devices, per_device(): asked = lax.all_to_all(asked, 'z', split_axis=0, concat_axis=0, tiled=True)  13.8 us
    all_to_all x1, starting transfers between devices, per_device(): lax.all_to_all(outgoing.reshape(nz * plane, 2 * slots, columns), PEERS, s...  9.98 us
    all_to_all x1, waiting for transfers between devices, per_device(): asked = lax.all_to_all(asked, 'z', split_axis=0, concat_axis=0, tiled=True)  8.55 us
    pallas_call x1, Pallas kernels, gather_up(): pl.pallas_call(gather_up_kernel, out_shape=jax.ShapeDtypeStruct((blocks,...  4.04 us
    pallas_call x1, Pallas kernels, pick(): pl.pallas_call(pick_kernel, out_shape=jax.ShapeDtypeStruct((rows, width /...  3.91 us
  transfers between devices with their start and end apart: 2, of which 2 were waited for; matrix products, arithmetic and copies ran while one was open for 1% of the time, Pallas kernels for 2%

profile of v1, /device:TPU:1, one launch (start us, length us, event | category | flops | bytes accessed | tf_op | source)
XLA Modules:
  0.0 121.9 jit_solution(8740584657618417026)
XLA Ops:
  0.0 0.9 reshape.30
  0.9 0.2 copy.11
  1.2 16.9 %all_to_all.15 = s32[32,2,16]{2,1,0:T(2,128)S(1)} all-to-all(s32[32,2,16]{2,1,0:T(2,128)S(1)} %copy.12), channel_id=1, replica_groups=mesh['x'=4,'y'=4,'z'=16,'c'=2] {'x','y','c'}, dimensions={0} | all-to-all | bytes 8192 | tf_op jit(solution)/shard_map/all_to_all | solution.py:118
  18.1 0.7 copy.13
  18.8 0.0 copy-start.1
  18.8 13.8 %all-to-all-start.1 = ((s32[16,1,64]{2,1,0:T(1,128)}), s32[16,1,64]{2,1,0:T(1,128)S(1)}, u32[]{:S(2)}, u32[]{:S(2)}) async-start(s32[16,1,64]{2,1,0:T(1,128)} %copy.13), calls=%async_computation.1 | async-start | bytes 16384 | tf_op jit(solution)/shard_map/all_to_all | solution.py:120
  32.6 0.0 copy-done.1
  32.6 0.2 reshape.34
  32.8 0.3 copy.15
  33.1 2.3 %weigh.1.table_ref = bf16[1024,256]{1,0:T(8,128)(2,1)} custom-call(f32[1024,128]{1,0:T(8,128)} %amplitudes_ref.1, s32[1024,128]{1,0:T(8,128)} %orbit_ref.3), custom_call_target="tpu_custom_call" | custom-call | flops 1048576 | bytes 1572864 | tf_op jit(solution)/shard_map/weigh/pallas_call | solution.py:35
  35.3 8.5 %all-to-all-done.1 = s32[16,1,64]{2,1,0:T(1,128)S(1)} async-done(((s32[16,1,64]{2,1,0:T(1,128)}), s32[16,1,64]{2,1,0:T(1,128)S(1)}, u32[]{:S(2)}, u32[]{:S(2)}) %all-to-all-start.1) | async-done | bytes 4128 | tf_op jit(solution)/shard_map/all_to_all | solution.py:120
  43.9 0.1 copy.14
  44.0 0.1 pad_add_fusion.1
  44.0 0.7 copy.16.index_ref
  44.7 3.9 %pick.1 = f32[2048,128]{1,0:T(8,128)} custom-call(s32[16,128]{1,0:T(8,128)} %copy.16.index_ref, bf16[1024,256]{1,0:T(8,128)(2,1)} %weigh.1.table_ref), custom_call_target="tpu_custom_call" | custom-call | flops 1073741824 | bytes 1572864 | tf_op jit(solution)/shard_map/pick/pallas_call | solution.py:67
  48.6 10.0 %all-to-all-start.2 = ((f32[512,4,128]{2,1,0:T(4,128)}), f32[512,4,128]{2,1,0:T(4,128)S(1)}, u32[]{:S(2)}, u32[]{:S(2)}) async-start(f32[512,4,128]{2,1,0:T(4,128)} %bitcast.17), calls=%async_computation.2 | async-start | bytes 2097152 | tf_op jit(solution)/shard_map/all_to_all | solution.py:128
  58.6 0.7 copy.17.index_ref
  59.3 57.6 %all-to-all-done.2 = f32[512,4,128]{2,1,0:T(4,128)S(1)} async-done(((f32[512,4,128]{2,1,0:T(4,128)}), f32[512,4,128]{2,1,0:T(4,128)S(1)}, u32[]{:S(2)}, u32[]{:S(2)}) %all-to-all-start.2) | async-done | bytes 1048608 | tf_op jit(solution)/shard_map/all_to_all | solution.py:128
  116.9 0.0 copy-start
  116.9 1.0 copy-done
  117.8 4.0 %gather_up.1 = f32[1024,128]{1,0:T(8,128)} custom-call(s32[16,128]{1,0:T(8,128)} %copy.17.index_ref, f32[2048,128]{1,0:T(8,128)} %bitcast.16, s32[1024,128]{1,0:T(8,128)} %orbit_ref.3), custom_call_target="tpu_custom_call" | custom-call | flops 1073741824 | bytes 2097152 | tf_op jit(solution)/shard_map/gather_up/pallas_call | solution.py:98
  (1 shorter events, 0.0 us)
Async XLA Ops:
  18.8 13.8 %copy-start.1 = (s32[1,512,2]{1,2,0:T(2,128)S(1)}, s32[1,512,2]{1,2,0:T(2,128)}, u32[]{:S(2)}) copy-start(s32[1,512,2]{1,2,0:T(2,128)} %param.7) | copy-start | bytes 12292
  18.8 25.1 %all-to-all-start.1 = ((s32[16,1,64]{2,1,0:T(1,128)}), s32[16,1,64]{2,1,0:T(1,128)S(1)}, u32[]{:S(2)}, u32[]{:S(2)}) async-start(s32[16,1,64]{2,1,0:T(1,128)} %copy.13), calls=%async_computation.1 | async-start | bytes 16384 | tf_op jit(solution)/shard_map/all_to_all | solution.py:120
  48.6 68.2 %all-to-all-start.2 = ((f32[512,4,128]{2,1,0:T(4,128)}), f32[512,4,128]{2,1,0:T(4,128)S(1)}, u32[]{:S(2)}, u32[]{:S(2)}) async-start(f32[512,4,128]{2,1,0:T(4,128)} %bitcast.17), calls=%async_computation.2 | async-start | bytes 2097152 | tf_op jit(solution)/shard_map/all_to_all | solution.py:128
  116.9 1.0 copy-start

commit v2 on v1

v2 whole, which is shorter than its diff:
```python
import jax
import jax.numpy as jnp
from jax import lax
from jax.experimental import pallas as pl
from jax.experimental.pallas import tpu as pltpu
from jax.sharding import Mesh
from jax.sharding import PartitionSpec as P

AXES = ("x", "y", "z", "c")
PEERS = ("z", "x", "y", "c")
PLANE = ("x", "y", "c")
IN_VMEM = pl.BlockSpec(memory_space=pltpu.VMEM)
MIB = 2**20
STEP = 8


def orbit_factor(orbit):
    return jnp.sqrt(96.0 * jnp.exp2(-orbit.astype(jnp.float32)))


def two_parts(values):
    high = values.astype(jnp.bfloat16)
    low = (values - high.astype(jnp.float32)).astype(jnp.bfloat16)
    return jnp.concatenate([high, low], axis=1)


def halves_added(product):
    columns = product.shape[1] // 2
    return product[:, :columns] + product[:, columns:]


def ones_where(hit):
    return jnp.where(hit, 1.0, 0.0).astype(jnp.bfloat16)


def picked(numbers, table, slots, step):
    lines, width = numbers.shape
    blocks = table.shape[0]
    columns = numbers.T
    block = lax.broadcasted_iota(jnp.int32, (width, blocks), 1)
    for slot in range(slots):
        for first in range(0, lines // slots, step):
            chosen = [
                ones_where(columns[:, row : row + 1] == block)
                for row in range(first * slots + slot, (first + step) * slots + slot, slots)
            ]
            product = jnp.dot(
                jnp.concatenate(chosen, axis=0), table, preferred_element_type=jnp.float32
            )
            yield slot, first * width, halves_added(product)


def own_kernel(slots, amplitudes_ref, orbit_ref, places_ref, table_ref, own_ref):
    table_ref[...] = two_parts(amplitudes_ref[...] * orbit_factor(orbit_ref[...]))
    peers = own_ref.shape[0] // slots
    for slot, first, rows in picked(places_ref[...], table_ref[...], slots, STEP):
        start = slot * peers + first
        own_ref[start : start + rows.shape[0], :] = rows


def own_rows(amplitudes, orbit, places, slots):
    blocks, columns = amplitudes.shape
    rows = places.size
    return pl.pallas_call(
        lambda *refs: own_kernel(slots, *refs),
        out_shape=(
            jax.ShapeDtypeStruct((blocks, 2 * columns), jnp.bfloat16),
            jax.ShapeDtypeStruct((rows, columns), jnp.float32),
        ),
        in_specs=[IN_VMEM] * 3,
        out_specs=(IN_VMEM, IN_VMEM),
        compiler_params=pltpu.CompilerParams(vmem_limit_bytes=16 * MIB),
        cost_estimate=pl.CostEstimate(
            flops=4 * rows * blocks * columns,
            bytes_accessed=20 * blocks * columns,
            transcendentals=blocks * columns,
        ),
        name="own_rows",
    )(amplitudes, orbit, places)


def serve_kernel(slots, wanted_ref, table_ref, own_ref, out_ref):
    peers = own_ref.shape[0] // slots
    for slot in range(slots):
        part = slice(slot * peers, (slot + 1) * peers)
        out_ref[pl.ds(slot, peers, stride=2 * slots), :] = own_ref[part, :]
    for slot, first, rows in picked(wanted_ref[...], table_ref[...], slots, STEP):
        start = first * 2 * slots + slots + slot
        out_ref[pl.ds(start, rows.shape[0], stride=2 * slots), :] = rows


def serve(wanted, table, own, slots):
    rows, columns = own.shape
    blocks = table.shape[0]
    return pl.pallas_call(
        lambda *refs: serve_kernel(slots, *refs),
        out_shape=jax.ShapeDtypeStruct((2 * rows, columns), jnp.float32),
        in_specs=[IN_VMEM] * 3,
        out_specs=IN_VMEM,
        compiler_params=pltpu.CompilerParams(vmem_limit_bytes=16 * MIB),
        cost_estimate=pl.CostEstimate(
            flops=4 * rows * blocks * columns,
            bytes_accessed=16 * rows * columns,
            transcendentals=0,
        ),
        name="serve",
    )(wanted, table, own)


def add_up_kernel(kinds, index_ref, rows_ref, orbit_ref, out_ref):
    groups, lanes = index_ref.shape
    blocks = out_ref.shape[0]
    peers = rows_ref.shape[0] // kinds
    rows = jnp.concatenate([two_parts(rows_ref[pl.ds(k, peers, stride=kinds), :]) for k in range(kinds)], axis=0)
    step = 128
    block = lax.broadcasted_iota(jnp.int32, (step, lanes), 0)
    for start in range(0, blocks, step):
        marks = jnp.concatenate([ones_where(block + start == index_ref[g : g + 1, :]) for g in range(groups)], axis=1)
        product = jnp.dot(marks, rows, preferred_element_type=jnp.float32)
        part = slice(start, start + step)
        out_ref[part, :] = halves_added(product) / orbit_factor(orbit_ref[part, :])


def add_up(index, rows, orbit, kinds):
    blocks, columns = orbit.shape
    count = rows.shape[0]
    return pl.pallas_call(
        lambda *refs: add_up_kernel(kinds, *refs),
        out_shape=jax.ShapeDtypeStruct((blocks, columns), jnp.float32),
        in_specs=[IN_VMEM] * 3,
        out_specs=IN_VMEM,
        compiler_params=pltpu.CompilerParams(vmem_limit_bytes=16 * MIB),
        cost_estimate=pl.CostEstimate(
            flops=4 * count * blocks * columns,
            bytes_accessed=(count + 2 * blocks) * columns * 4,
            transcendentals=blocks * columns,
        ),
        name="add_up",
    )(index, rows, orbit)


def per_device(amplitudes, orbit_index, requests, targets):
    columns = amplitudes.shape[1]
    nx, ny, nz, nc = (lax.axis_size(a) for a in AXES)
    plane = nx * ny * nc
    slots = requests.shape[-1]
    asked = requests.reshape(nx, ny, nz, nc, slots).transpose(0, 1, 3, 4, 2)
    asked = asked.reshape(plane, slots, nz)
    asked = lax.all_to_all(asked, PLANE, split_axis=0, concat_axis=0, tiled=True)
    asked = asked.transpose(2, 1, 0)
    wanted = lax.all_to_all(asked, "z", split_axis=0, concat_axis=0, tiled=True)
    places = targets.reshape(nx, ny, nz, nc, slots).transpose(2, 4, 0, 1, 3)
    places = places.reshape(nz, slots, plane)
    table, own = own_rows(
        amplitudes, orbit_index, places.reshape(nz * slots, plane), slots
    )
    outgoing = serve(wanted.reshape(nz * slots, plane), table, own, slots)
    arrived = lax.all_to_all(
        outgoing.reshape(nz * plane, 2 * slots, columns),
        PEERS,
        split_axis=0,
        concat_axis=0,
        tiled=True,
    )
    landing = jnp.concatenate([wanted, places], axis=1).transpose(1, 0, 2)
    return add_up(
        landing.reshape(-1, 128), arrived.reshape(-1, columns), orbit_index, 2 * slots
    )


def solution(mesh):
    groups, shards = mesh.devices.shape
    devices = mesh.devices.reshape(groups, 4, shards // 8, 2)
    split = P(AXES)
    return jax.shard_map(
        per_device,
        mesh=Mesh(devices, AXES),
        in_specs=(split, split, split, split),
        out_specs=split,
        check_vma=False,
    )
```

time: 122 us -> 117 us (0.959)
  blocking collectives: 16.9 us -> 0 us
  starting transfers between devices: 23.8 us -> 33.5 us
  waiting for transfers between devices: 66.1 us -> 74.9 us
  Pallas kernels: 10.2 us -> 4.94 us
    all_to_all x1 -> x0, blocking collectives: 16.9 us -> none  [per_device(): lax.all_to_all(asked, PLANE, split_axis=0, concat_axis=0, tiled=True)]
    all_to_all x1 -> x2, starting transfers between devices: 13.8 us -> 23.5 us  [the longest x1 13 us: per_device(): wanted = lax.all_to_all(asked, 'z', split_axis=0, concat_axis=0, tiled=True)]
    all_to_all x1 -> x2, waiting for transfers between devices: 8.55 us -> 17.2 us  [the longest x1 10.4 us: per_device(): wanted = lax.all_to_all(asked, 'z', split_axis=0, concat_axis=0, tiled=True)]
    pallas_call x3, Pallas kernels: 10.2 us -> 4.94 us  [the longest x1 2.15 us: add_up(): pl.pallas_call(lambda *refs: add_up_kernel(kinds, *refs), out_shape=jax.S...]
    reshape x4 -> x2, local copies, waits for them, and re-layouts: 2.21 us -> 0.28 us  [the longest x1 0.2 us: per_device(): places = targets.reshape(nx, ny, nz, nc, slots).transpose(2, 4, 0, 1, 3)]
  transfers between devices with their start and end apart: 2 -> 3, of which waited for: 2 -> 3; matrix products, arithmetic and copies ran while one was open for 1% -> 1% of each run, Pallas kernels for 2% -> 1%
where the time goes in v2:
time: 117 us
  waiting for transfers between devices  74.9 us (64%)
  starting transfers between devices  33.5 us (29%)
  Pallas kernels  4.94 us (4%)
  local copies, waits for them, and re-layouts  3.52 us (3%)
    all_to_all x1, waiting for transfers between devices, per_device(): lax.all_to_all(outgoing.reshape(nz * plane, 2 * slots, columns), PEERS, s...  57.7 us
    all_to_all x1, starting transfers between devices, per_device(): wanted = lax.all_to_all(asked, 'z', split_axis=0, concat_axis=0, tiled=True)  13 us
    all_to_all x1, starting transfers between devices, per_device(): lax.all_to_all(asked, PLANE, split_axis=0, concat_axis=0, tiled=True)  10.5 us
    all_to_all x1, waiting for transfers between devices, per_device(): wanted = lax.all_to_all(asked, 'z', split_axis=0, concat_axis=0, tiled=True)  10.4 us
    all_to_all x1, starting transfers between devices, per_device(): lax.all_to_all(outgoing.reshape(nz * plane, 2 * slots, columns), PEERS, s...  10 us
    all_to_all x1, waiting for transfers between devices, per_device(): lax.all_to_all(asked, PLANE, split_axis=0, concat_axis=0, tiled=True)  6.79 us
  transfers between devices with their start and end apart: 3, of which 3 were waited for; matrix products, arithmetic and copies ran while one was open for 1% of the time, Pallas kernels for 1%

profile of v2, /device:TPU:1, one launch (start us, length us, event | category | flops | bytes accessed | tf_op | source)
XLA Modules:
  0.0 117.1 jit_solution(4215878375530994882)
XLA Ops:
  0.0 0.9 reshape.24
  0.9 0.2 copy.15
  1.1 0.7 copy.16
  1.8 0.0 copy-start.2
  1.8 10.5 %all-to-all-start = ((s32[32,2,16]{2,1,0:T(2,128)}), s32[32,2,16]{2,1,0:T(2,128)S(1)}, u32[]{:S(2)}, u32[]{:S(2)}) async-start(s32[32,2,16]{2,1,0:T(2,128)} %copy.16), calls=%async_computation | async-start | bytes 65536 | tf_op jit(solution)/shard_map/all_to_all | solution.py:149
  12.3 0.0 copy-done.2
  12.3 0.0 copy-start
  12.4 0.0 copy-start.1
  12.4 0.2 reshape.26
  12.6 0.1 copy.23
  12.7 0.2 reshape.32.refs_2_
  12.9 6.8 %all-to-all-done = s32[32,2,16]{2,1,0:T(2,128)S(1)} async-done(((s32[32,2,16]{2,1,0:T(2,128)}), s32[32,2,16]{2,1,0:T(2,128)S(1)}, u32[]{:S(2)}, u32[]{:S(2)}) %all-to-all-start) | async-done | bytes 4128 | tf_op jit(solution)/shard_map/all_to_all | solution.py:149
  19.7 0.7 copy.17
  20.4 13.0 %all-to-all-start.1 = ((s32[16,2,32]{2,1,0:T(2,128)}), s32[16,2,32]{2,1,0:T(2,128)S(1)}, u32[]{:S(2)}, u32[]{:S(2)}) async-start(s32[16,2,32]{2,1,0:T(2,128)} %copy.17), calls=%async_computation.1 | async-start | bytes 32768 | tf_op jit(solution)/shard_map/all_to_all | solution.py:151
  33.4 0.0 copy-done
  33.4 0.0 copy-done.1
  33.4 1.0 own_rows.1
  34.4 10.4 %all-to-all-done.1 = s32[16,2,32]{2,1,0:T(2,128)S(1)} async-done(((s32[16,2,32]{2,1,0:T(2,128)}), s32[16,2,32]{2,1,0:T(2,128)S(1)}, u32[]{:S(2)}, u32[]{:S(2)}) %all-to-all-start.1) | async-done | bytes 4128 | tf_op jit(solution)/shard_map/all_to_all | solution.py:151
  44.8 1.8 %serve.1 = f32[2048,128]{1,0:T(8,128)} custom-call(s32[32,32]{1,0:T(8,128)S(1)} %bitcast.15, bf16[1024,256]{1,0:T(8,128)(2,1)S(1)} %get-tuple-element.7.refs_1_, f32[1024,128]{1,0:T(8,128)S(1)} %get-tuple-element.8.refs_2_), custom_call_target="tpu_custom_call" | custom-call | flops 536870912 | bytes 2097152 | tf_op jit(solution)/shard_map/serve/pallas_call | solution.py:95
  46.6 10.0 %all-to-all-start.2 = ((f32[512,4,128]{2,1,0:T(4,128)}), f32[512,4,128]{2,1,0:T(4,128)S(1)}, u32[]{:S(2)}, u32[]{:S(2)}) async-start(f32[512,4,128]{2,1,0:T(4,128)} %bitcast.7), calls=%async_computation.2 | async-start | bytes 2097152 | tf_op jit(solution)/shard_map/all_to_all | solution.py:158
  56.6 0.2 copy.18
  56.9 0.1 copy.19
  57.0 0.1 copy.20
  57.1 0.1 reshape.28.refs_0_
  57.2 57.7 %all-to-all-done.2 = f32[512,4,128]{2,1,0:T(4,128)S(1)} async-done(((f32[512,4,128]{2,1,0:T(4,128)}), f32[512,4,128]{2,1,0:T(4,128)S(1)}, u32[]{:S(2)}, u32[]{:S(2)}) %all-to-all-start.2) | async-done | bytes 1048608 | tf_op jit(solution)/shard_map/all_to_all | solution.py:158
  114.9 2.2 %add_up.1 = f32[1024,128]{1,0:T(8,128)} custom-call(s32[16,128]{1,0:T(8,128)S(1)} %reshape.28.refs_0_, f32[2048,128]{1,0:T(8,128)S(1)} %bitcast.14, s32[1024,128]{1,0:T(8,128)S(1)} %copy-done.1), custom_call_target="tpu_custom_call" | custom-call | flops 1073741824 | bytes 2097152 | tf_op jit(solution)/shard_map/add_up/pallas_call | solution.py:127
  (1 shorter events, 0.0 us)
Async XLA Ops:
  1.8 10.5 %copy-start.2 = (s32[1,512,2]{1,2,0:T(2,128)S(1)}, s32[1,512,2]{1,2,0:T(2,128)}, u32[]{:S(2)}) copy-start(s32[1,512,2]{1,2,0:T(2,128)} %param.7) | copy-start | bytes 12292
  1.8 17.9 %all-to-all-start = ((s32[32,2,16]{2,1,0:T(2,128)}), s32[32,2,16]{2,1,0:T(2,128)S(1)}, u32[]{:S(2)}, u32[]{:S(2)}) async-start(s32[32,2,16]{2,1,0:T(2,128)} %copy.16), calls=%async_computation | async-start | bytes 65536 | tf_op jit(solution)/shard_map/all_to_all | solution.py:149
  12.3 21.1 %copy-start = (f32[1024,128]{1,0:T(8,128)S(1)}, f32[1024,128]{1,0:T(8,128)}, u32[]{:S(2)}) copy-start(f32[1024,128]{1,0:T(8,128)} %refs_0_.1) | copy-start | bytes 1572868
  12.4 21.1 %copy-start.1 = (s32[1024,128]{1,0:T(8,128)S(1)}, s32[1024,128]{1,0:T(8,128)}, u32[]{:S(2)}) copy-start(s32[1024,128]{1,0:T(8,128)} %refs_2_.1) | copy-start | bytes 1572868
  20.4 24.4 %all-to-all-start.1 = ((s32[16,2,32]{2,1,0:T(2,128)}), s32[16,2,32]{2,1,0:T(2,128)S(1)}, u32[]{:S(2)}, u32[]{:S(2)}) async-start(s32[16,2,32]{2,1,0:T(2,128)} %copy.17), calls=%async_computation.1 | async-start | bytes 32768 | tf_op jit(solution)/shard_map/all_to_all | solution.py:151
  46.6 68.3 %all-to-all-start.2 = ((f32[512,4,128]{2,1,0:T(4,128)}), f32[512,4,128]{2,1,0:T(4,128)S(1)}, u32[]{:S(2)}, u32[]{:S(2)}) async-start(f32[512,4,128]{2,1,0:T(4,128)} %bitcast.7), calls=%async_computation.2 | async-start | bytes 2097152 | tf_op jit(solution)/shard_map/all_to_all | solution.py:158

commit v3 on v2

v3 whole, which is shorter than its diff:
```python
import jax
import jax.numpy as jnp
from jax import lax
from jax.experimental import pallas as pl
from jax.experimental.pallas import tpu as pltpu
from jax.sharding import Mesh
from jax.sharding import PartitionSpec as P

AXES = ("x", "y", "z", "c")
PEERS = ("z", "c", "x", "y")
PLANE = ("c", "x", "y")
IN_VMEM = pl.BlockSpec(memory_space=pltpu.VMEM)
MIB = 2**20
STEP = 8


def orbit_factor(orbit):
    return jnp.sqrt(96.0 * jnp.exp2(-orbit.astype(jnp.float32)))


def two_parts(values):
    high = values.astype(jnp.bfloat16)
    low = (values - high.astype(jnp.float32)).astype(jnp.bfloat16)
    return jnp.concatenate([high, low], axis=1)


def halves_added(product):
    columns = product.shape[1] // 2
    return product[:, :columns] + product[:, columns:]


def ones_where(hit):
    return jnp.where(hit, 1.0, 0.0).astype(jnp.bfloat16)


def lanes_joined(pieces, lanes):
    share = lanes // pieces[0].shape[1]
    rows = [
        jnp.concatenate(pieces[start : start + share], axis=1)
        for start in range(0, len(pieces), share)
    ]
    return jnp.concatenate(rows, axis=0)


def every_other(values, first):
    lanes = values.shape[1]
    lane = lax.broadcasted_iota(jnp.int32, values.shape, 1)
    if first:
        values = pltpu.roll(values, lanes - 1, 1)
    for bit in range(4):
        moved = pltpu.roll(values, lanes - (1 << bit), 1)
        values = jnp.where((lane >> bit) & 1 == 1, moved, values)
    return values


def deal_kernel(asked_ref, out_ref):
    slots, total = asked_ref.shape
    peers, _, lines = out_ref.shape
    columns = peers // 2
    run = total // columns
    for start in range(0, total, 128):
        whole = asked_ref[:, start : start + 128]
        for core in range(2):
            sorted_out = every_other(whole, core)
            for part in range(0, 128, run):
                column = (start + part) // run
                out_ref[core * columns + column] = sorted_out[:, part : part + lines]


def deal(asked, peers, lines):
    slots = asked.shape[0]
    return pl.pallas_call(
        deal_kernel,
        out_shape=jax.ShapeDtypeStruct((peers, slots, lines), jnp.int32),
        in_specs=[IN_VMEM],
        out_specs=IN_VMEM,
        compiler_params=pltpu.CompilerParams(vmem_limit_bytes=4 * MIB),
        cost_estimate=pl.CostEstimate(flops=40960, bytes_accessed=40960, transcendentals=0),
        name="deal",
    )(asked)


def picked(columns, table, step):
    width = columns[0].shape[0]
    blocks = table.shape[0]
    block = lax.broadcasted_iota(jnp.int32, (width, blocks), 1)
    for first in range(0, len(columns), step):
        chosen = [ones_where(column == block) for column in columns[first : first + step]]
        product = jnp.dot(
            jnp.concatenate(chosen, axis=0), table, preferred_element_type=jnp.float32
        )
        yield first * width, halves_added(product)


def own_kernel(amplitudes_ref, orbit_ref, places_ref, table_ref, own_ref, landing_ref):
    table_ref[...] = two_parts(amplitudes_ref[...] * orbit_factor(orbit_ref[...]))
    slots, total = places_ref.shape
    run = 32
    lanes = landing_ref.shape[1]
    columns = []
    for slot in range(slots):
        grid = jnp.concatenate(
            [places_ref[slot : slot + 1, start : start + run] for start in range(0, total, run)],
            axis=0,
        )
        columns += [grid[:, column : column + 1] for column in range(run)]
        turned = grid.T
        share = total // lanes
        landing_ref[slot * share : (slot + 1) * share, :] = lanes_joined(
            [turned[row : row + 1, :] for row in range(run)], lanes
        )
    for first, rows in picked(columns, table_ref[...], 16):
        own_ref[first : first + rows.shape[0], :] = rows


def own_rows(amplitudes, orbit, places):
    blocks, columns = amplitudes.shape
    rows = places.size
    return pl.pallas_call(
        own_kernel,
        out_shape=(
            jax.ShapeDtypeStruct((blocks, 2 * columns), jnp.bfloat16),
            jax.ShapeDtypeStruct((rows, columns), jnp.float32),
            jax.ShapeDtypeStruct((rows // 128, 128), jnp.int32),
        ),
        in_specs=[IN_VMEM] * 3,
        out_specs=(IN_VMEM,) * 3,
        compiler_params=pltpu.CompilerParams(vmem_limit_bytes=16 * MIB),
        cost_estimate=pl.CostEstimate(
            flops=4 * rows * blocks * columns,
            bytes_accessed=20 * blocks * columns,
            transcendentals=blocks * columns,
        ),
        name="own_rows",
    )(amplitudes, orbit, places)


def serve_kernel(wanted_ref, table_ref, own_ref, out_ref, landing_ref):
    lines, slots, width = wanted_ref.shape
    lanes = landing_ref.shape[1]
    peers = lines * width
    share = peers // lanes
    for slot in range(slots):
        part = slice(slot * peers, (slot + 1) * peers)
        out_ref[pl.ds(slot, peers, stride=2 * slots), :] = own_ref[part, :]
    numbers = [wanted_ref[:, slot, :] for slot in range(slots)]
    turned = [number.T for number in numbers]
    columns = [turn[:, line : line + 1] for turn in turned for line in range(lines)]
    for first, rows in picked(columns, table_ref[...], 8):
        slot, start = divmod(first, peers)
        out_ref[
            pl.ds(start * 2 * slots + slots + slot, rows.shape[0], stride=2 * slots), :
        ] = rows
    for slot in range(slots):
        landing_ref[slot * share : (slot + 1) * share, :] = lanes_joined(
            [numbers[slot][line : line + 1, :] for line in range(lines)], lanes
        )


def serve(wanted, table, own):
    rows, columns = own.shape
    blocks = table.shape[0]
    return pl.pallas_call(
        serve_kernel,
        out_shape=(
            jax.ShapeDtypeStruct((2 * rows, columns), jnp.float32),
            jax.ShapeDtypeStruct((rows // 128, 128), jnp.int32),
        ),
        in_specs=[IN_VMEM] * 3,
        out_specs=(IN_VMEM,) * 2,
        compiler_params=pltpu.CompilerParams(vmem_limit_bytes=16 * MIB),
        cost_estimate=pl.CostEstimate(
            flops=4 * rows * blocks * columns,
            bytes_accessed=16 * rows * columns,
            transcendentals=0,
        ),
        name="serve",
    )(wanted, table, own)


def add_up_kernel(first_ref, second_ref, rows_ref, orbit_ref, out_ref):
    groups, lanes = first_ref.shape
    blocks = out_ref.shape[0]
    count = rows_ref.shape[0]
    peers = groups * lanes // 2
    kinds = count // peers
    rows = jnp.concatenate(
        [two_parts(rows_ref[pl.ds(kind, peers, stride=kinds), :]) for kind in range(kinds)],
        axis=0,
    )
    index = [ref[group : group + 1, :] for ref in (first_ref, second_ref) for group in range(groups)]
    step = 128
    block = lax.broadcasted_iota(jnp.int32, (step, lanes), 0)
    for start in range(0, blocks, step):
        marks = jnp.concatenate(
            [ones_where(block + start == numbers) for numbers in index], axis=1
        )
        product = jnp.dot(marks, rows, preferred_element_type=jnp.float32)
        part = slice(start, start + step)
        out_ref[part, :] = halves_added(product) / orbit_factor(orbit_ref[part, :])


def add_up(first, second, rows, orbit):
    blocks, columns = orbit.shape
    count = rows.shape[0]
    return pl.pallas_call(
        add_up_kernel,
        out_shape=jax.ShapeDtypeStruct((blocks, columns), jnp.float32),
        in_specs=[IN_VMEM] * 4,
        out_specs=IN_VMEM,
        compiler_params=pltpu.CompilerParams(vmem_limit_bytes=16 * MIB),
        cost_estimate=pl.CostEstimate(
            flops=4 * count * blocks * columns,
            bytes_accessed=(count + 2 * blocks) * columns * 4,
            transcendentals=blocks * columns,
        ),
        name="add_up",
    )(first, second, rows, orbit)


def per_device(amplitudes, orbit_index, requests, targets):
    columns = amplitudes.shape[1]
    nx, ny, nz, nc = (lax.axis_size(a) for a in AXES)
    plane = nx * ny * nc
    slots = requests.shape[-1]
    asked = deal(requests.reshape(-1, slots).T, plane, nz)
    asked = lax.all_to_all(asked, PLANE, split_axis=0, concat_axis=0, tiled=True)
    wanted = lax.all_to_all(
        asked.transpose(2, 1, 0), "z", split_axis=0, concat_axis=0, tiled=True
    )
    table, own, landing = own_rows(amplitudes, orbit_index, targets.reshape(-1, slots).T)
    outgoing, wanted_landing = serve(wanted, table, own)
    arrived = lax.all_to_all(
        outgoing.reshape(nz * plane, 2 * slots, columns),
        PEERS,
        split_axis=0,
        concat_axis=0,
        tiled=True,
    )
    return add_up(wanted_landing, landing, arrived.reshape(-1, columns), orbit_index)


def solution(mesh):
    groups, shards = mesh.devices.shape
    devices = mesh.devices.reshape(groups, 4, shards // 8, 2)
    split = P(AXES)
    return jax.shard_map(
        per_device,
        mesh=Mesh(devices, AXES),
        in_specs=(split, split, split, split),
        out_specs=split,
        check_vma=False,
    )
```

time: 117 us -> 116 us (level)
  blocking collectives: 0 us -> 85.2 us
  waiting for transfers between devices: 74.9 us -> 8.31 us
  starting transfers between devices: 33.5 us -> 13.9 us
    all_to_all x0 -> x2, blocking collectives: none -> 85.2 us  [the longest x1 68.6 us: per_device(): lax.all_to_all(outgoing.reshape(nz * plane, 2 * slots, columns), PEERS, s...]
    all_to_all x3 -> x1, waiting for transfers between devices: 74.9 us -> 8.31 us  [per_device(): lax.all_to_all(asked.transpose(2, 1, 0), 'z', split_axis=0, concat_axis=0...]
    all_to_all x3 -> x1, starting transfers between devices: 33.5 us -> 13.9 us  [per_device(): lax.all_to_all(asked.transpose(2, 1, 0), 'z', split_axis=0, concat_axis=0...]
    unnamed x6 -> x10, local copies, waits for them, and re-layouts: 0.02 us -> 2.77 us
    reshape x4 -> x0, local copies, waits for them, and re-layouts: 1.83 us -> none  [the longest x1 0.89 us: per_device(): asked = requests.reshape(nx, ny, nz, nc, slots).transpose(0, 1, 3, 4, 2)]
    transpose x4 -> x0, local copies, waits for them, and re-layouts: 1.25 us -> none  [the longest x1 0.68 us: per_device(): asked = asked.transpose(2, 1, 0)]
    pallas_call x3 -> x4, Pallas kernels: 4.94 us -> 4.46 us  [the longest x1 2.15 us: add_up(): pl.pallas_call(add_up_kernel, out_shape=jax.ShapeDtypeStruct((blocks, col...]
  transfers between devices with their start and end apart: 3 -> 1, of which waited for: 3 -> 1; matrix products, arithmetic and copies ran while one was open for 1% -> 0% of each run, Pallas kernels for 1% -> 1%
where the time goes in v3:
time: 116 us; the launch traced here: 115 us
  blocking collectives  85.2 us (73%)
  starting transfers between devices  13.9 us (12%)
  waiting for transfers between devices  8.31 us (7%)
  Pallas kernels  4.46 us (4%)
  local copies, waits for them, and re-layouts  3.46 us (3%)
    all_to_all x1, blocking collectives, per_device(): lax.all_to_all(outgoing.reshape(nz * plane, 2 * slots, columns), PEERS, s...  68.6 us
    all_to_all x1, blocking collectives, per_device(): lax.all_to_all(asked, PLANE, split_axis=0, concat_axis=0, tiled=True)  16.6 us
    all_to_all x1, starting transfers between devices, per_device(): lax.all_to_all(asked.transpose(2, 1, 0), 'z', split_axis=0, concat_axis=0...  13.9 us
    all_to_all x1, waiting for transfers between devices, per_device(): lax.all_to_all(asked.transpose(2, 1, 0), 'z', split_axis=0, concat_axis=0...  8.31 us
    unnamed x10, local copies, waits for them, and re-layouts  2.77 us
  transfers between devices with their start and end apart: 1, of which 1 were waited for; matrix products, arithmetic and copies ran while one was open for 0% of the time, Pallas kernels for 1%

profile of v3, /device:TPU:1, one launch (start us, length us, event | category | flops | bytes accessed | tf_op | source)
XLA Modules:
  0.0 115.3 jit_solution(11015016390194507783)
XLA Ops:
  0.0 0.0 copy-start
  0.0 0.7 copy-done
  0.7 0.4 deal.1
  1.1 16.6 %all_to_all.15 = s32[32,2,16]{2,1,0:T(2,128)S(1)} all-to-all(s32[32,2,16]{2,1,0:T(2,128)S(1)} %deal.1), channel_id=1, replica_groups=mesh['x'=4,'y'=4,'z'=16,'c'=2] {'c','x','y'}, dimensions={0} | all-to-all | bytes 8192 | tf_op jit(solution)/shard_map/all_to_all | solution.py:227
  17.7 0.7 copy.8
  18.4 0.0 copy-start.4
  18.4 13.9 %all-to-all-start.1 = ((s32[16,2,32]{2,1,0:T(2,128)}), s32[16,2,32]{2,1,0:T(2,128)S(1)}, u32[]{:S(2)}, u32[]{:S(2)}) async-start(s32[16,2,32]{2,1,0:T(2,128)} %bitcast.2), calls=%async_computation.1 | async-start | bytes 32768 | tf_op jit(solution)/shard_map/all_to_all | solution.py:228
  32.2 0.0 copy-done.4
  32.2 0.0 copy-start.1
  32.3 1.0 copy-done.1
  33.3 0.0 copy-start.2
  33.3 1.0 copy-done.2
  34.3 1.0 own_rows.1
  35.3 8.3 %all-to-all-done.1.wanted_ref = s32[16,2,32]{2,1,0:T(2,128)S(1)} async-done(((s32[16,2,32]{2,1,0:T(2,128)}), s32[16,2,32]{2,1,0:T(2,128)S(1)}, u32[]{:S(2)}, u32[]{:S(2)}) %all-to-all-start.1) | async-done | bytes 4128 | tf_op jit(solution)/shard_map/all_to_all | solution.py:228
  43.6 0.9 serve.1
  44.6 0.0 copy-start.3
  44.6 68.6 %all_to_all.16 = f32[512,4,128]{2,1,0:T(4,128)S(1)} all-to-all(f32[512,4,128]{2,1,0:T(4,128)S(1)} %bitcast.9), channel_id=1, replica_groups=mesh['x'=4,'y'=4,'z'=16,'c'=2] {'z','c','x','y'}, dimensions={0} | all-to-all | bytes 2097152 | tf_op jit(solution)/shard_map/all_to_all | solution.py:233
  113.2 0.0 copy-done.3
  113.2 2.2 %add_up.1 = f32[1024,128]{1,0:T(8,128)} custom-call(s32[8,128]{1,0:T(8,128)S(1)} %get-tuple-element.12.first_ref, s32[8,128]{1,0:T(8,128)S(1)} %get-tuple-element.13.second_ref, f32[2048,128]{1,0:T(8,128)S(1)} %bitcast.10, s32[1024,128]{1,0:T(8,128)S(1)} %copy-done.3), custom_call_target="tpu_custom_call" | custom-call | flops 1073741824 | bytes 2097152 | tf_op jit(solution)/shard_map/add_up/pallas_call | solution.py:206
Async XLA Ops:
  0.0 0.7 copy-start
  18.4 13.9 %copy-start.4 = (s32[1,512,2]{1,2,0:T(2,128)S(1)}, s32[1,512,2]{1,2,0:T(2,128)}, u32[]{:S(2)}) copy-start(s32[1,512,2]{1,2,0:T(2,128)} %param.7) | copy-start | bytes 12292
  18.4 25.3 %all-to-all-start.1 = ((s32[16,2,32]{2,1,0:T(2,128)}), s32[16,2,32]{2,1,0:T(2,128)S(1)}, u32[]{:S(2)}, u32[]{:S(2)}) async-start(s32[16,2,32]{2,1,0:T(2,128)} %bitcast.2), calls=%async_computation.1 | async-start | bytes 32768 | tf_op jit(solution)/shard_map/all_to_all | solution.py:228
  32.2 1.0 copy-start.1
  33.3 1.0 copy-start.2
  44.6 68.6 %copy-start.3 = (s32[1024,128]{1,0:T(8,128)S(1)}, s32[1024,128]{1,0:T(8,128)}, u32[]{:S(2)}) copy-start(s32[1024,128]{1,0:T(8,128)} %orbit_ref.3) | copy-start | bytes 1572868

commit v4 on v3

--- a/solution.py
+++ b/solution.py
@@ -30,7 +30,7 @@
 
 
 def ones_where(hit):
-    return jnp.where(hit, 1.0, 0.0).astype(jnp.bfloat16)
+    return jnp.where(hit, jnp.bfloat16(1.0), jnp.bfloat16(0.0))
 
 
 def lanes_joined(pieces, lanes):
@@ -83,17 +83,17 @@
 def picked(columns, table, step):
     width = columns[0].shape[0]
     blocks = table.shape[0]
-    block = lax.broadcasted_iota(jnp.int32, (width, blocks), 1)
+    block = lax.broadcasted_iota(jnp.int32, (width, blocks), 1).astype(jnp.int16)
     for first in range(0, len(columns), step):
-        chosen = [ones_where(column == block) for column in columns[first : first + step]]
+        chosen = [ones_where(column.astype(jnp.int16) == block) for column in columns[first : first + step]]
         product = jnp.dot(
             jnp.concatenate(chosen, axis=0), table, preferred_element_type=jnp.float32
         )
         yield first * width, halves_added(product)
 
 
-def own_kernel(amplitudes_ref, orbit_ref, places_ref, table_ref, own_ref, landing_ref):
-    table_ref[...] = two_parts(amplitudes_ref[...] * orbit_factor(orbit_ref[...]))
+def own_kernel(weighted_ref, places_ref, table_ref, own_ref, landing_ref):
+    table_ref[...] = two_parts(weighted_ref[...])
     slots, total = places_ref.shape
     run = 32
     lanes = landing_ref.shape[1]
@@ -113,8 +113,8 @@
         own_ref[first : first + rows.shape[0], :] = rows
 
 
-def own_rows(amplitudes, orbit, places):
-    blocks, columns = amplitudes.shape
+def own_rows(weighted, places):
+    blocks, columns = weighted.shape
     rows = places.size
     return pl.pallas_call(
         own_kernel,
@@ -123,16 +123,16 @@
             jax.ShapeDtypeStruct((rows, columns), jnp.float32),
             jax.ShapeDtypeStruct((rows // 128, 128), jnp.int32),
         ),
-        in_specs=[IN_VMEM] * 3,
+        in_specs=[IN_VMEM] * 2,
         out_specs=(IN_VMEM,) * 3,
         compiler_params=pltpu.CompilerParams(vmem_limit_bytes=16 * MIB),
         cost_estimate=pl.CostEstimate(
             flops=4 * rows * blocks * columns,
-            bytes_accessed=20 * blocks * columns,
-            transcendentals=blocks * columns,
+            bytes_accessed=16 * blocks * columns,
+            transcendentals=0,
         ),
         name="own_rows",
-    )(amplitudes, orbit, places)
+    )(weighted, places)
 
 
 def serve_kernel(wanted_ref, table_ref, own_ref, out_ref, landing_ref):
@@ -189,11 +189,12 @@
         axis=0,
     )
     index = [ref[group : group + 1, :] for ref in (first_ref, second_ref) for group in range(groups)]
-    step = 128
+    step = 256
     block = lax.broadcasted_iota(jnp.int32, (step, lanes), 0)
+    index = [jnp.broadcast_to(numbers, (step, lanes)).astype(jnp.int16) for numbers in index]
     for start in range(0, blocks, step):
         marks = jnp.concatenate(
-            [ones_where(block + start == numbers) for numbers in index], axis=1
+            [ones_where((block + start).astype(jnp.int16) == numbers) for numbers in index], axis=1
         )
         product = jnp.dot(marks, rows, preferred_element_type=jnp.float32)
         part = slice(start, start + step)
@@ -228,7 +229,8 @@
     wanted = lax.all_to_all(
         asked.transpose(2, 1, 0), "z", split_axis=0, concat_axis=0, tiled=True
     )
-    table, own, landing = own_rows(amplitudes, orbit_index, targets.reshape(-1, slots).T)
+    weighted = amplitudes * orbit_factor(orbit_index)
+    table, own, landing = own_rows(weighted, targets.reshape(-1, slots).T)
     outgoing, wanted_landing = serve(wanted, table, own)
     arrived = lax.all_to_all(
         outgoing.reshape(nz * plane, 2 * slots, columns),

time: 116 us -> 116 us (level)
  blocking collectives: 85.2 us -> 68.6 us
  starting transfers between devices: 13.9 us -> 23.7 us
  waiting for transfers between devices: 8.31 us -> 16.1 us
  local copies, waits for them, and re-layouts: 3.46 us -> 1.38 us
  other arithmetic: 0 us -> 1.43 us
    all_to_all x1 -> x0, blocking collectives: 16.6 us -> none  [per_device(): lax.all_to_all(asked, PLANE, split_axis=0, concat_axis=0, tiled=True)]
    all_to_all x0 -> x1, starting transfers between devices: none -> 10.5 us  [per_device(): lax.all_to_all(asked, PLANE, split_axis=0, concat_axis=0, tiled=True)]
    all_to_all x0 -> x1, waiting for transfers between devices: none -> 5.54 us  [per_device(): lax.all_to_all(asked, PLANE, split_axis=0, concat_axis=0, tiled=True)]
    all_to_all x1, waiting for transfers between devices: 8.31 us -> 10.5 us  [per_device(): lax.all_to_all(asked.transpose(2, 1, 0), 'z', split_axis=0, concat_axis=0...]
    unnamed x10 -> x6, local copies, waits for them, and re-layouts: 2.77 us -> 0.7 us
    mul x0 -> x1, other arithmetic: none -> 1.43 us  [per_device(): weighted = amplitudes * orbit_factor(orbit_index)]
  transfers between devices with their start and end apart: 1 -> 2, of which waited for: 1 -> 2; matrix products, arithmetic and copies ran while one was open for 0% -> 1% of each run, Pallas kernels for 1% -> 1%
where the time goes in v4:
time: 116 us
  blocking collectives  68.6 us (59%)
  starting transfers between devices  23.7 us (20%)
  waiting for transfers between devices  16.1 us (14%)
  Pallas kernels  4.82 us (4%)
  other arithmetic  1.43 us (1%)
  local copies, waits for them, and re-layouts  1.38 us (1%)
    all_to_all x1, blocking collectives, per_device(): lax.all_to_all(outgoing.reshape(nz * plane, 2 * slots, columns), PEERS, s...  68.6 us
    all_to_all x1, starting transfers between devices, per_device(): lax.all_to_all(asked.transpose(2, 1, 0), 'z', split_axis=0, concat_axis=0...  13.2 us
    all_to_all x1, waiting for transfers between devices, per_device(): lax.all_to_all(asked.transpose(2, 1, 0), 'z', split_axis=0, concat_axis=0...  10.5 us
    all_to_all x1, starting transfers between devices, per_device(): lax.all_to_all(asked, PLANE, split_axis=0, concat_axis=0, tiled=True)  10.5 us
    all_to_all x1, waiting for transfers between devices, per_device(): lax.all_to_all(asked, PLANE, split_axis=0, concat_axis=0, tiled=True)  5.54 us
  transfers between devices with their start and end apart: 2, of which 2 were waited for; matrix products, arithmetic and copies ran while one was open for 1% of the time, Pallas kernels for 1%

profile of v4, /device:TPU:1, one launch (start us, length us, event | category | flops | bytes accessed | tf_op | source)
XLA Modules:
  0.0 116.0 jit_solution(5768362201747777188)
XLA Ops:
  0.0 0.0 copy-start.1
  0.0 0.7 copy-done.1
  0.7 1.0 deal.1
  1.7 10.5 %all-to-all-start = ((s32[32,2,16]{2,1,0:T(2,128)}), s32[32,2,16]{2,1,0:T(2,128)S(1)}, u32[]{:S(2)}, u32[]{:S(2)}) async-start(s32[32,2,16]{2,1,0:T(2,128)} %deal.1), calls=%async_computation | async-start | bytes 65536 | tf_op jit(solution)/shard_map/all_to_all | solution.py:228
  12.2 1.4 %sqrt_multiply_fusion.weighted_ref = f32[1024,128]{1,0:T(8,128)S(1)} fusion(f32[1024,128]{1,0:T(8,128)} %param.4, s32[1024,128]{1,0:T(8,128)} %orbit_ref.1), kind=kLoop, calls=%fused_computation | loop fusion | flops 655360 | bytes 1572864 | tf_op jit(solution)/shard_map/mul | solution.py:232
  13.7 5.5 %all-to-all-done = s32[32,2,16]{2,1,0:T(2,128)S(1)} async-done(((s32[32,2,16]{2,1,0:T(2,128)}), s32[32,2,16]{2,1,0:T(2,128)S(1)}, u32[]{:S(2)}, u32[]{:S(2)}) %all-to-all-start) | async-done | bytes 4128 | tf_op jit(solution)/shard_map/all_to_all | solution.py:228
  19.2 0.7 copy.8
  19.9 0.0 copy-start.2
  19.9 13.2 %all-to-all-start.1 = ((s32[16,2,32]{2,1,0:T(2,128)}), s32[16,2,32]{2,1,0:T(2,128)S(1)}, u32[]{:S(2)}, u32[]{:S(2)}) async-start(s32[16,2,32]{2,1,0:T(2,128)} %bitcast.2), calls=%async_computation.1 | async-start | bytes 32768 | tf_op jit(solution)/shard_map/all_to_all | solution.py:229
  33.1 0.0 copy-done.2
  33.1 0.8 own_rows.1
  33.9 10.5 %all-to-all-done.1.wanted_ref = s32[16,2,32]{2,1,0:T(2,128)S(1)} async-done(((s32[16,2,32]{2,1,0:T(2,128)}), s32[16,2,32]{2,1,0:T(2,128)S(1)}, u32[]{:S(2)}, u32[]{:S(2)}) %all-to-all-start.1) | async-done | bytes 4128 | tf_op jit(solution)/shard_map/all_to_all | solution.py:229
  44.5 0.8 serve.1
  45.3 0.0 copy-start
  45.3 68.6 %all_to_all.15 = f32[512,4,128]{2,1,0:T(4,128)S(1)} all-to-all(f32[512,4,128]{2,1,0:T(4,128)S(1)} %bitcast.9), channel_id=1, replica_groups=mesh['x'=4,'y'=4,'z'=16,'c'=2] {'z','c','x','y'}, dimensions={0} | all-to-all | bytes 2097152 | tf_op jit(solution)/shard_map/all_to_all | solution.py:235
  113.9 0.0 copy-done
  113.9 2.1 %add_up.1 = f32[1024,128]{1,0:T(8,128)} custom-call(s32[8,128]{1,0:T(8,128)S(1)} %get-tuple-element.12.first_ref, s32[8,128]{1,0:T(8,128)S(1)} %get-tuple-element.13.second_ref, f32[2048,128]{1,0:T(8,128)S(1)} %bitcast.10, s32[1024,128]{1,0:T(8,128)S(1)} %copy-done), custom_call_target="tpu_custom_call" | custom-call | flops 1073741824 | bytes 2097152 | tf_op jit(solution)/shard_map/add_up/pallas_call | solution.py:207
Async XLA Ops:
  0.0 0.7 copy-start.1
  1.7 17.5 %all-to-all-start = ((s32[32,2,16]{2,1,0:T(2,128)}), s32[32,2,16]{2,1,0:T(2,128)S(1)}, u32[]{:S(2)}, u32[]{:S(2)}) async-start(s32[32,2,16]{2,1,0:T(2,128)} %deal.1), calls=%async_computation | async-start | bytes 65536 | tf_op jit(solution)/shard_map/all_to_all | solution.py:228
  19.9 13.2 %copy-start.2 = (s32[1,512,2]{1,2,0:T(2,128)S(1)}, s32[1,512,2]{1,2,0:T(2,128)}, u32[]{:S(2)}) copy-start(s32[1,512,2]{1,2,0:T(2,128)} %param.7) | copy-start | bytes 12292
  19.9 24.6 %all-to-all-start.1 = ((s32[16,2,32]{2,1,0:T(2,128)}), s32[16,2,32]{2,1,0:T(2,128)S(1)}, u32[]{:S(2)}, u32[]{:S(2)}) async-start(s32[16,2,32]{2,1,0:T(2,128)} %bitcast.2), calls=%async_computation.1 | async-start | bytes 32768 | tf_op jit(solution)/shard_map/all_to_all | solution.py:229
  45.3 68.6 %copy-start = (s32[1024,128]{1,0:T(8,128)S(1)}, s32[1024,128]{1,0:T(8,128)}, u32[]{:S(2)}) copy-start(s32[1024,128]{1,0:T(8,128)} %orbit_ref.1) | copy-start | bytes 1572868

commit v5 on v3

--- a/solution.py
+++ b/solution.py
@@ -30,7 +30,7 @@
 
 
 def ones_where(hit):
-    return jnp.where(hit, 1.0, 0.0).astype(jnp.bfloat16)
+    return jnp.where(hit, jnp.bfloat16(1.0), jnp.bfloat16(0.0))
 
 
 def lanes_joined(pieces, lanes):
@@ -83,9 +83,9 @@
 def picked(columns, table, step):
     width = columns[0].shape[0]
     blocks = table.shape[0]
-    block = lax.broadcasted_iota(jnp.int32, (width, blocks), 1)
+    block = lax.broadcasted_iota(jnp.int32, (width, blocks), 1).astype(jnp.int16)
     for first in range(0, len(columns), step):
-        chosen = [ones_where(column == block) for column in columns[first : first + step]]
+        chosen = [ones_where(column.astype(jnp.int16) == block) for column in columns[first : first + step]]
         product = jnp.dot(
             jnp.concatenate(chosen, axis=0), table, preferred_element_type=jnp.float32
         )
@@ -189,11 +189,12 @@
         axis=0,
     )
     index = [ref[group : group + 1, :] for ref in (first_ref, second_ref) for group in range(groups)]
-    step = 128
+    step = 256
     block = lax.broadcasted_iota(jnp.int32, (step, lanes), 0)
+    index = [jnp.broadcast_to(numbers, (step, lanes)).astype(jnp.int16) for numbers in index]
     for start in range(0, blocks, step):
         marks = jnp.concatenate(
-            [ones_where(block + start == numbers) for numbers in index], axis=1
+            [ones_where((block + start).astype(jnp.int16) == numbers) for numbers in index], axis=1
         )
         product = jnp.dot(marks, rows, preferred_element_type=jnp.float32)
         part = slice(start, start + step)

time: 116 us -> 116 us (level)
  no operation moved by 1% of the time
where the time goes in v5:
time: 116 us; the launch traced here: 115 us
  blocking collectives  85.2 us (73%)
  starting transfers between devices  13.9 us (12%)
  waiting for transfers between devices  8.42 us (7%)
  Pallas kernels  4.23 us (4%)
  local copies, waits for them, and re-layouts  3.46 us (3%)
    all_to_all x1, blocking collectives, per_device(): lax.all_to_all(outgoing.reshape(nz * plane, 2 * slots, columns), PEERS, s...  68.6 us
    all_to_all x1, blocking collectives, per_device(): lax.all_to_all(asked, PLANE, split_axis=0, concat_axis=0, tiled=True)  16.6 us
    all_to_all x1, starting transfers between devices, per_device(): lax.all_to_all(asked.transpose(2, 1, 0), 'z', split_axis=0, concat_axis=0...  13.9 us
    all_to_all x1, waiting for transfers between devices, per_device(): lax.all_to_all(asked.transpose(2, 1, 0), 'z', split_axis=0, concat_axis=0...  8.42 us
    unnamed x10, local copies, waits for them, and re-layouts  2.77 us
  transfers between devices with their start and end apart: 1, of which 1 were waited for; matrix products, arithmetic and copies ran while one was open for 0% of the time, Pallas kernels for 1%

profile of v5, /device:TPU:1, one launch (start us, length us, event | category | flops | bytes accessed | tf_op | source)
XLA Modules:
  0.0 115.2 jit_solution(16474823856879286198)
XLA Ops:
  0.0 0.0 copy-start
  0.0 0.7 copy-done
  0.7 0.4 deal.1
  1.1 16.6 %all_to_all.15 = s32[32,2,16]{2,1,0:T(2,128)S(1)} all-to-all(s32[32,2,16]{2,1,0:T(2,128)S(1)} %deal.1), channel_id=1, replica_groups=mesh['x'=4,'y'=4,'z'=16,'c'=2] {'c','x','y'}, dimensions={0} | all-to-all | bytes 8192 | tf_op jit(solution)/shard_map/all_to_all | solution.py:228
  17.7 0.7 copy.8
  18.4 0.0 copy-start.4
  18.4 13.9 %all-to-all-start.1 = ((s32[16,2,32]{2,1,0:T(2,128)}), s32[16,2,32]{2,1,0:T(2,128)S(1)}, u32[]{:S(2)}, u32[]{:S(2)}) async-start(s32[16,2,32]{2,1,0:T(2,128)} %bitcast.2), calls=%async_computation.1 | async-start | bytes 32768 | tf_op jit(solution)/shard_map/all_to_all | solution.py:229
  32.2 0.0 copy-done.4
  32.2 0.0 copy-start.1
  32.3 1.0 copy-done.1
  33.3 0.0 copy-start.2
  33.3 1.0 copy-done.2
  34.3 0.9 own_rows.1
  35.2 8.4 %all-to-all-done.1.wanted_ref = s32[16,2,32]{2,1,0:T(2,128)S(1)} async-done(((s32[16,2,32]{2,1,0:T(2,128)}), s32[16,2,32]{2,1,0:T(2,128)S(1)}, u32[]{:S(2)}, u32[]{:S(2)}) %all-to-all-start.1) | async-done | bytes 4128 | tf_op jit(solution)/shard_map/all_to_all | solution.py:229
  43.6 0.8 serve.1
  44.5 0.0 copy-start.3
  44.5 68.6 %all_to_all.16 = f32[512,4,128]{2,1,0:T(4,128)S(1)} all-to-all(f32[512,4,128]{2,1,0:T(4,128)S(1)} %bitcast.9), channel_id=1, replica_groups=mesh['x'=4,'y'=4,'z'=16,'c'=2] {'z','c','x','y'}, dimensions={0} | all-to-all | bytes 2097152 | tf_op jit(solution)/shard_map/all_to_all | solution.py:234
  113.1 0.0 copy-done.3
  113.1 2.1 %add_up.1 = f32[1024,128]{1,0:T(8,128)} custom-call(s32[8,128]{1,0:T(8,128)S(1)} %get-tuple-element.12.first_ref, s32[8,128]{1,0:T(8,128)S(1)} %get-tuple-element.13.second_ref, f32[2048,128]{1,0:T(8,128)S(1)} %bitcast.10, s32[1024,128]{1,0:T(8,128)S(1)} %copy-done.3), custom_call_target="tpu_custom_call" | custom-call | flops 1073741824 | bytes 2097152 | tf_op jit(solution)/shard_map/add_up/pallas_call | solution.py:207
Async XLA Ops:
  0.0 0.7 copy-start
  18.4 13.9 %copy-start.4 = (s32[1,512,2]{1,2,0:T(2,128)S(1)}, s32[1,512,2]{1,2,0:T(2,128)}, u32[]{:S(2)}) copy-start(s32[1,512,2]{1,2,0:T(2,128)} %param.7) | copy-start | bytes 12292
  18.4 25.3 %all-to-all-start.1 = ((s32[16,2,32]{2,1,0:T(2,128)}), s32[16,2,32]{2,1,0:T(2,128)S(1)}, u32[]{:S(2)}, u32[]{:S(2)}) async-start(s32[16,2,32]{2,1,0:T(2,128)} %bitcast.2), calls=%async_computation.1 | async-start | bytes 32768 | tf_op jit(solution)/shard_map/all_to_all | solution.py:229
  32.2 1.0 copy-start.1
  33.3 1.0 copy-start.2
  44.5 68.6 %copy-start.3 = (s32[1024,128]{1,0:T(8,128)S(1)}, s32[1024,128]{1,0:T(8,128)}, u32[]{:S(2)}) copy-start(s32[1024,128]{1,0:T(8,128)} %orbit_ref.3) | copy-start | bytes 1572868

commit v6 on v5

--- a/solution.py
+++ b/solution.py
@@ -42,36 +42,29 @@
     return jnp.concatenate(rows, axis=0)
 
 
-def every_other(values, first):
-    lanes = values.shape[1]
-    lane = lax.broadcasted_iota(jnp.int32, values.shape, 1)
-    if first:
-        values = pltpu.roll(values, lanes - 1, 1)
-    for bit in range(4):
-        moved = pltpu.roll(values, lanes - (1 << bit), 1)
-        values = jnp.where((lane >> bit) & 1 == 1, moved, values)
-    return values
-
-
 def deal_kernel(asked_ref, out_ref):
     slots, total = asked_ref.shape
-    peers, _, lines = out_ref.shape
-    columns = peers // 2
-    run = total // columns
-    for start in range(0, total, 128):
-        whole = asked_ref[:, start : start + 128]
-        for core in range(2):
-            sorted_out = every_other(whole, core)
-            for part in range(0, 128, run):
-                column = (start + part) // run
-                out_ref[core * columns + column] = sorted_out[:, part : part + lines]
-
-
-def deal(asked, peers, lines):
-    slots = asked.shape[0]
+    lines, _, width = out_ref.shape
+    run = 32
+    for slot in range(slots):
+        grid = jnp.concatenate(
+            [asked_ref[slot : slot + 1, start : start + run] for start in range(0, total, run)],
+            axis=0,
+        )
+        turned = grid.T
+        cores = run // lines
+        for line in range(lines):
+            out_ref[line, slot : slot + 1, :] = jnp.concatenate(
+                [turned[line * cores + core : line * cores + core + 1, :] for core in range(cores)],
+                axis=1,
+            )
+
+
+def deal(asked, lines):
+    slots, total = asked.shape
     return pl.pallas_call(
         deal_kernel,
-        out_shape=jax.ShapeDtypeStruct((peers, slots, lines), jnp.int32),
+        out_shape=jax.ShapeDtypeStruct((lines, slots, total // lines), jnp.int32),
         in_specs=[IN_VMEM],
         out_specs=IN_VMEM,
         compiler_params=pltpu.CompilerParams(vmem_limit_bytes=4 * MIB),
@@ -136,15 +129,17 @@
 
 
 def serve_kernel(wanted_ref, table_ref, own_ref, out_ref, landing_ref):
-    lines, slots, width = wanted_ref.shape
+    width, slots, lines = wanted_ref.shape
     lanes = landing_ref.shape[1]
     peers = lines * width
     share = peers // lanes
     for slot in range(slots):
         part = slice(slot * peers, (slot + 1) * peers)
         out_ref[pl.ds(slot, peers, stride=2 * slots), :] = own_ref[part, :]
-    numbers = [wanted_ref[:, slot, :] for slot in range(slots)]
-    turned = [number.T for number in numbers]
+    whole = jnp.concatenate([wanted_ref[:, slot, :] for slot in range(slots)], axis=1)
+    square = whole.T
+    numbers = [square[slot * lines : (slot + 1) * lines, :] for slot in range(slots)]
+    turned = [whole[:, slot * lines : (slot + 1) * lines] for slot in range(slots)]
     columns = [turn[:, line : line + 1] for turn in turned for line in range(lines)]
     for first, rows in picked(columns, table_ref[...], 8):
         slot, start = divmod(first, peers)
@@ -224,10 +219,10 @@
     nx, ny, nz, nc = (lax.axis_size(a) for a in AXES)
     plane = nx * ny * nc
     slots = requests.shape[-1]
-    asked = deal(requests.reshape(-1, slots).T, plane, nz)
-    asked = lax.all_to_all(asked, PLANE, split_axis=0, concat_axis=0, tiled=True)
+    asked = deal(requests.reshape(-1, slots).T, nz)
+    asked = lax.all_to_all(asked, "z", split_axis=0, concat_axis=0, tiled=True)
     wanted = lax.all_to_all(
-        asked.transpose(2, 1, 0), "z", split_axis=0, concat_axis=0, tiled=True
+        asked.transpose(2, 1, 0), PLANE, split_axis=0, concat_axis=0, tiled=True
     )
     table, own, landing = own_rows(amplitudes, orbit_index, targets.reshape(-1, slots).T)
     outgoing, wanted_landing = serve(wanted, table, own)

time: 116 us -> 115 us (level)
  blocking collectives: 85.2 us -> 94.1 us
  starting transfers between devices: 13.9 us -> 9.3 us
  waiting for transfers between devices: 8.42 us -> 4.03 us
    all_to_all x1, blocking collectives: 16.6 us -> 26.9 us  [per_device(): asked = lax.all_to_all(asked, 'z', split_axis=0, concat_axis=0, tiled=True)]
    all_to_all x1, starting transfers between devices: 13.9 us -> 9.3 us  [per_device(): lax.all_to_all(asked.transpose(2, 1, 0), PLANE, split_axis=0, concat_axis...]
    all_to_all x1, waiting for transfers between devices: 8.42 us -> 4.03 us  [per_device(): lax.all_to_all(asked.transpose(2, 1, 0), PLANE, split_axis=0, concat_axis...]
    all_to_all x1, blocking collectives: 68.6 us -> 67.2 us  [per_device(): lax.all_to_all(outgoing.reshape(nz * plane, 2 * slots, columns), PEERS, s...]
where the time goes in v6:
time: 115 us
  blocking collectives  94.1 us (82%)
  starting transfers between devices  9.3 us (8%)
  Pallas kernels  4.05 us (4%)
  waiting for transfers between devices  4.03 us (4%)
  local copies, waits for them, and re-layouts  3.47 us (3%)
    all_to_all x1, blocking collectives, per_device(): lax.all_to_all(outgoing.reshape(nz * plane, 2 * slots, columns), PEERS, s...  67.2 us
    all_to_all x1, blocking collectives, per_device(): asked = lax.all_to_all(asked, 'z', split_axis=0, concat_axis=0, tiled=True)  26.9 us
    all_to_all x1, starting transfers between devices, per_device(): lax.all_to_all(asked.transpose(2, 1, 0), PLANE, split_axis=0, concat_axis...  9.3 us
    all_to_all x1, waiting for transfers between devices, per_device(): lax.all_to_all(asked.transpose(2, 1, 0), PLANE, split_axis=0, concat_axis...  4.03 us
    unnamed x10, local copies, waits for them, and re-layouts  2.77 us
  transfers between devices with their start and end apart: 1, of which 1 were waited for; matrix products, arithmetic and copies ran while one was open for 0% of the time, Pallas kernels for 1%

profile of v6, /device:TPU:1, one launch (start us, length us, event | category | flops | bytes accessed | tf_op | source)
XLA Modules:
  0.0 115.0 jit_solution(12084772570336890542)
XLA Ops:
  0.0 0.0 copy-start
  0.0 0.7 copy-done
  0.7 0.2 deal.1
  0.9 26.9 %all_to_all.15 = s32[16,2,32]{2,1,0:T(2,128)S(1)} all-to-all(s32[16,2,32]{2,1,0:T(2,128)S(1)} %deal.1), channel_id=1, replica_groups=mesh['x'=4,'y'=4,'z'=16,'c'=2] {'z'}, dimensions={0} | all-to-all | bytes 8192 | tf_op jit(solution)/shard_map/all_to_all | solution.py:223
  27.9 0.7 copy.6
  28.6 0.0 copy-start.4
  28.6 9.3 %all-to-all-start.1 = ((s32[32,2,16]{2,1,0:T(2,128)}), s32[32,2,16]{2,1,0:T(2,128)S(1)}, u32[]{:S(2)}, u32[]{:S(2)}) async-start(s32[32,2,16]{2,1,0:T(2,128)} %bitcast.2), calls=%async_computation.1 | async-start | bytes 65536 | tf_op jit(solution)/shard_map/all_to_all | solution.py:224
  37.9 0.0 copy-done.4
  37.9 0.0 copy-start.1
  37.9 1.0 copy-done.1
  38.9 0.0 copy-start.2
  38.9 1.0 copy-done.2
  40.0 0.9 own_rows.1
  40.8 4.0 %all-to-all-done.1.wanted_ref = s32[32,2,16]{2,1,0:T(2,128)S(1)} async-done(((s32[32,2,16]{2,1,0:T(2,128)}), s32[32,2,16]{2,1,0:T(2,128)S(1)}, u32[]{:S(2)}, u32[]{:S(2)}) %all-to-all-start.1) | async-done | bytes 4128 | tf_op jit(solution)/shard_map/all_to_all | solution.py:224
  44.9 0.8 serve.1
  45.7 0.0 copy-start.3
  45.7 67.2 %all_to_all.16 = f32[512,4,128]{2,1,0:T(4,128)S(1)} all-to-all(f32[512,4,128]{2,1,0:T(4,128)S(1)} %bitcast.9), channel_id=1, replica_groups=mesh['x'=4,'y'=4,'z'=16,'c'=2] {'z','c','x','y'}, dimensions={0} | all-to-all | bytes 2097152 | tf_op jit(solution)/shard_map/all_to_all | solution.py:229
  112.9 0.0 copy-done.3
  112.9 2.1 %add_up.1 = f32[1024,128]{1,0:T(8,128)} custom-call(s32[8,128]{1,0:T(8,128)S(1)} %get-tuple-element.12.first_ref, s32[8,128]{1,0:T(8,128)S(1)} %get-tuple-element.13.second_ref, f32[2048,128]{1,0:T(8,128)S(1)} %bitcast.10, s32[1024,128]{1,0:T(8,128)S(1)} %copy-done.3), custom_call_target="tpu_custom_call" | custom-call | flops 1073741824 | bytes 2097152 | tf_op jit(solution)/shard_map/add_up/pallas_call | solution.py:202
Async XLA Ops:
  0.0 0.7 copy-start
  28.6 9.3 %copy-start.4 = (s32[1,512,2]{1,2,0:T(2,128)S(1)}, s32[1,512,2]{1,2,0:T(2,128)}, u32[]{:S(2)}) copy-start(s32[1,512,2]{1,2,0:T(2,128)} %param.7) | copy-start | bytes 12292
  28.6 16.3 %all-to-all-start.1 = ((s32[32,2,16]{2,1,0:T(2,128)}), s32[32,2,16]{2,1,0:T(2,128)S(1)}, u32[]{:S(2)}, u32[]{:S(2)}) async-start(s32[32,2,16]{2,1,0:T(2,128)} %bitcast.2), calls=%async_computation.1 | async-start | bytes 65536 | tf_op jit(solution)/shard_map/all_to_all | solution.py:224
  37.9 1.0 copy-start.1
  38.9 1.0 copy-start.2
  45.7 67.2 %copy-start.3 = (s32[1024,128]{1,0:T(8,128)S(1)}, s32[1024,128]{1,0:T(8,128)}, u32[]{:S(2)}) copy-start(s32[1024,128]{1,0:T(8,128)} %orbit_ref.3) | copy-start | bytes 1572868

commit v7 on v6

--- a/solution.py
+++ b/solution.py
@@ -85,8 +85,8 @@
         yield first * width, halves_added(product)
 
 
-def own_kernel(amplitudes_ref, orbit_ref, places_ref, table_ref, own_ref, landing_ref):
-    table_ref[...] = two_parts(amplitudes_ref[...] * orbit_factor(orbit_ref[...]))
+def own_kernel(weighted_ref, places_ref, table_ref, own_ref, landing_ref):
+    table_ref[...] = two_parts(weighted_ref[...])
     slots, total = places_ref.shape
     run = 32
     lanes = landing_ref.shape[1]
@@ -106,8 +106,8 @@
         own_ref[first : first + rows.shape[0], :] = rows
 
 
-def own_rows(amplitudes, orbit, places):
-    blocks, columns = amplitudes.shape
+def own_rows(weighted, places):
+    blocks, columns = weighted.shape
     rows = places.size
     return pl.pallas_call(
         own_kernel,
@@ -116,16 +116,16 @@
             jax.ShapeDtypeStruct((rows, columns), jnp.float32),
             jax.ShapeDtypeStruct((rows // 128, 128), jnp.int32),
         ),
-        in_specs=[IN_VMEM] * 3,
+        in_specs=[IN_VMEM] * 2,
         out_specs=(IN_VMEM,) * 3,
         compiler_params=pltpu.CompilerParams(vmem_limit_bytes=16 * MIB),
         cost_estimate=pl.CostEstimate(
-            flops=4 * rows * blocks * columns,
-            bytes_accessed=20 * blocks * columns,
-            transcendentals=blocks * columns,
+            flops=rows * columns,
+            bytes_accessed=rows * columns,
+            transcendentals=0,
         ),
         name="own_rows",
-    )(amplitudes, orbit, places)
+    )(weighted, places)
 
 
 def serve_kernel(wanted_ref, table_ref, own_ref, out_ref, landing_ref):
@@ -224,7 +224,8 @@
     wanted = lax.all_to_all(
         asked.transpose(2, 1, 0), PLANE, split_axis=0, concat_axis=0, tiled=True
     )
-    table, own, landing = own_rows(amplitudes, orbit_index, targets.reshape(-1, slots).T)
+    weighted = amplitudes * orbit_factor(orbit_index)
+    table, own, landing = own_rows(weighted, targets.reshape(-1, slots).T)
     outgoing, wanted_landing = serve(wanted, table, own)
     arrived = lax.all_to_all(
         outgoing.reshape(nz * plane, 2 * slots, columns),

time: 115 us -> 115 us (level)
  local copies, waits for them, and re-layouts: 3.47 us -> 1.39 us
  other arithmetic: 0 us -> 1.44 us
    unnamed x10 -> x6, local copies, waits for them, and re-layouts: 2.77 us -> 0.7 us
    mul x0 -> x1, other arithmetic: none -> 1.44 us  [per_device(): weighted = amplitudes * orbit_factor(orbit_index)]
  transfers between devices with their start and end apart: 1 -> 1, of which waited for: 1 -> 1; matrix products, arithmetic and copies ran while one was open for 0% -> 1% of each run, Pallas kernels for 1% -> 1%
where the time goes in v7:
time: 115 us
  blocking collectives  94.1 us (82%)
  starting transfers between devices  9.16 us (8%)
  waiting for transfers between devices  4.7 us (4%)
  Pallas kernels  4.01 us (3%)
  other arithmetic  1.44 us (1%)
  local copies, waits for them, and re-layouts  1.39 us (1%)
    all_to_all x1, blocking collectives, per_device(): lax.all_to_all(outgoing.reshape(nz * plane, 2 * slots, columns), PEERS, s...  67.2 us
    all_to_all x1, blocking collectives, per_device(): asked = lax.all_to_all(asked, 'z', split_axis=0, concat_axis=0, tiled=True)  26.9 us
    all_to_all x1, starting transfers between devices, per_device(): lax.all_to_all(asked.transpose(2, 1, 0), PLANE, split_axis=0, concat_axis...  9.16 us
    all_to_all x1, waiting for transfers between devices, per_device(): lax.all_to_all(asked.transpose(2, 1, 0), PLANE, split_axis=0, concat_axis...  4.7 us
  transfers between devices with their start and end apart: 1, of which 1 were waited for; matrix products, arithmetic and copies ran while one was open for 1% of the time, Pallas kernels for 1%

profile of v7, /device:TPU:1, one launch (start us, length us, event | category | flops | bytes accessed | tf_op | source)
XLA Modules:
  0.0 114.9 jit_solution(17119353043845797056)
XLA Ops:
  0.0 0.0 copy-start.2
  0.0 0.7 copy-done.2
  0.7 0.2 deal.1
  0.9 26.9 %all_to_all.15 = s32[16,2,32]{2,1,0:T(2,128)S(1)} all-to-all(s32[16,2,32]{2,1,0:T(2,128)S(1)} %deal.1), channel_id=1, replica_groups=mesh['x'=4,'y'=4,'z'=16,'c'=2] {'z'}, dimensions={0} | all-to-all | bytes 8192 | tf_op jit(solution)/shard_map/all_to_all | solution.py:223
  27.9 0.7 copy.6
  28.6 9.2 %all-to-all-start.1 = ((s32[32,2,16]{2,1,0:T(2,128)}), s32[32,2,16]{2,1,0:T(2,128)S(1)}, u32[]{:S(2)}, u32[]{:S(2)}) async-start(s32[32,2,16]{2,1,0:T(2,128)} %bitcast.2), calls=%async_computation.1 | async-start | bytes 65536 | tf_op jit(solution)/shard_map/all_to_all | solution.py:224
  37.7 0.0 copy-start.1
  37.7 1.4 %sqrt_multiply_fusion.weighted_ref = f32[1024,128]{1,0:T(8,128)S(1)} fusion(f32[1024,128]{1,0:T(8,128)} %param.4, s32[1024,128]{1,0:T(8,128)} %orbit_ref.1), kind=kLoop, calls=%fused_computation | loop fusion | flops 655360 | bytes 1572864 | tf_op jit(solution)/shard_map/mul | solution.py:227
  39.2 0.0 copy-done.1
  39.2 0.8 own_rows.1
  40.0 4.7 %all-to-all-done.1.wanted_ref = s32[32,2,16]{2,1,0:T(2,128)S(1)} async-done(((s32[32,2,16]{2,1,0:T(2,128)}), s32[32,2,16]{2,1,0:T(2,128)S(1)}, u32[]{:S(2)}, u32[]{:S(2)}) %all-to-all-start.1) | async-done | bytes 4128 | tf_op jit(solution)/shard_map/all_to_all | solution.py:224
  44.7 0.8 serve.1
  45.6 0.0 copy-start
  45.6 67.2 %all_to_all.16 = f32[512,4,128]{2,1,0:T(4,128)S(1)} all-to-all(f32[512,4,128]{2,1,0:T(4,128)S(1)} %bitcast.9), channel_id=1, replica_groups=mesh['x'=4,'y'=4,'z'=16,'c'=2] {'z','c','x','y'}, dimensions={0} | all-to-all | bytes 2097152 | tf_op jit(solution)/shard_map/all_to_all | solution.py:230
  112.8 0.0 copy-done
  112.8 2.1 %add_up.1 = f32[1024,128]{1,0:T(8,128)} custom-call(s32[8,128]{1,0:T(8,128)S(1)} %get-tuple-element.12.first_ref, s32[8,128]{1,0:T(8,128)S(1)} %get-tuple-element.13.second_ref, f32[2048,128]{1,0:T(8,128)S(1)} %bitcast.10, s32[1024,128]{1,0:T(8,128)S(1)} %copy-done), custom_call_target="tpu_custom_call" | custom-call | flops 1073741824 | bytes 2097152 | tf_op jit(solution)/shard_map/add_up/pallas_call | solution.py:202
Async XLA Ops:
  0.0 0.7 copy-start.2
  28.6 16.2 %all-to-all-start.1 = ((s32[32,2,16]{2,1,0:T(2,128)}), s32[32,2,16]{2,1,0:T(2,128)S(1)}, u32[]{:S(2)}, u32[]{:S(2)}) async-start(s32[32,2,16]{2,1,0:T(2,128)} %bitcast.2), calls=%async_computation.1 | async-start | bytes 65536 | tf_op jit(solution)/shard_map/all_to_all | solution.py:224
  37.7 1.5 %copy-start.1 = (s32[1,512,2]{1,2,0:T(2,128)S(1)}, s32[1,512,2]{1,2,0:T(2,128)}, u32[]{:S(2)}) copy-start(s32[1,512,2]{1,2,0:T(2,128)} %param.7) | copy-start | bytes 12292
  45.6 67.2 %copy-start = (s32[1024,128]{1,0:T(8,128)S(1)}, s32[1024,128]{1,0:T(8,128)}, u32[]{:S(2)}) copy-start(s32[1024,128]{1,0:T(8,128)} %orbit_ref.1) | copy-start | bytes 1572868

commit v8 on v6

--- a/solution.py
+++ b/solution.py
@@ -173,27 +173,37 @@
     )(wanted, table, own)
 
 
-def add_up_kernel(first_ref, second_ref, rows_ref, orbit_ref, out_ref):
+def add_up_kernel(first_ref, second_ref, rows_ref, orbit_ref, out_ref, held_ref, sent):
     groups, lanes = first_ref.shape
     blocks = out_ref.shape[0]
     count = rows_ref.shape[0]
     peers = groups * lanes // 2
     kinds = count // peers
-    rows = jnp.concatenate(
-        [two_parts(rows_ref[pl.ds(kind, peers, stride=kinds), :]) for kind in range(kinds)],
-        axis=0,
-    )
+    share = peers // lanes
     index = [ref[group : group + 1, :] for ref in (first_ref, second_ref) for group in range(groups)]
     step = 256
     block = lax.broadcasted_iota(jnp.int32, (step, lanes), 0)
     index = [jnp.broadcast_to(numbers, (step, lanes)).astype(jnp.int16) for numbers in index]
+    parts = {}
+    copies = []
     for start in range(0, blocks, step):
-        marks = jnp.concatenate(
-            [ones_where((block + start).astype(jnp.int16) == numbers) for numbers in index], axis=1
-        )
-        product = jnp.dot(marks, rows, preferred_element_type=jnp.float32)
+        here = (block + start).astype(jnp.int16)
+        total = None
+        for kind in range(kinds):
+            if kind not in parts:
+                parts[kind] = two_parts(rows_ref[pl.ds(kind, peers, stride=kinds), :])
+            marks = jnp.concatenate(
+                [ones_where(here == numbers) for numbers in index[kind * share : (kind + 1) * share]], axis=1
+            )
+            product = jnp.dot(marks, parts[kind], preferred_element_type=jnp.float32)
+            total = product if total is None else total + product
         part = slice(start, start + step)
-        out_ref[part, :] = halves_added(product) / orbit_factor(orbit_ref[part, :])
+        held_ref[part, :] = halves_added(total) / orbit_factor(orbit_ref[part, :])
+        copy = pltpu.make_async_copy(held_ref.at[part, :], out_ref.at[part, :], sent.at[start // step])
+        copy.start()
+        copies.append(copy)
+    for copy in copies:
+        copy.wait()
 
 
 def add_up(first, second, rows, orbit):
@@ -203,7 +213,11 @@
         add_up_kernel,
         out_shape=jax.ShapeDtypeStruct((blocks, columns), jnp.float32),
         in_specs=[IN_VMEM] * 4,
-        out_specs=IN_VMEM,
+        out_specs=pl.BlockSpec(memory_space=pl.ANY),
+        scratch_shapes=[
+            pltpu.VMEM((blocks, columns), jnp.float32),
+            pltpu.SemaphoreType.DMA((blocks // 256,)),
+        ],
         compiler_params=pltpu.CompilerParams(vmem_limit_bytes=16 * MIB),
         cost_estimate=pl.CostEstimate(
             flops=4 * count * blocks * columns,

time: 115 us -> 115 us (level)
  no operation moved by 1% of the time
where the time goes in v8:
time: 115 us
  blocking collectives  94.1 us (82%)
  starting transfers between devices  9.3 us (8%)
  waiting for transfers between devices  4.03 us (4%)
  Pallas kernels  4 us (3%)
  local copies, waits for them, and re-layouts  3.47 us (3%)
    all_to_all x1, blocking collectives, per_device(): lax.all_to_all(outgoing.reshape(nz * plane, 2 * slots, columns), PEERS, s...  67.2 us
    all_to_all x1, blocking collectives, per_device(): asked = lax.all_to_all(asked, 'z', split_axis=0, concat_axis=0, tiled=True)  26.9 us
    all_to_all x1, starting transfers between devices, per_device(): lax.all_to_all(asked.transpose(2, 1, 0), PLANE, split_axis=0, concat_axis...  9.3 us
    all_to_all x1, waiting for transfers between devices, per_device(): lax.all_to_all(asked.transpose(2, 1, 0), PLANE, split_axis=0, concat_axis...  4.03 us
    unnamed x10, local copies, waits for them, and re-layouts  2.77 us
  transfers between devices with their start and end apart: 1, of which 1 were waited for; matrix products, arithmetic and copies ran while one was open for 0% of the time, Pallas kernels for 1%

profile of v8, /device:TPU:1, one launch (start us, length us, event | category | flops | bytes accessed | tf_op | source)
XLA Modules:
  0.0 115.0 jit_solution(18433100749437212854)
XLA Ops:
  0.0 0.0 copy-start
  0.0 0.7 copy-done
  0.7 0.2 deal.1
  0.9 26.9 %all_to_all.15 = s32[16,2,32]{2,1,0:T(2,128)S(1)} all-to-all(s32[16,2,32]{2,1,0:T(2,128)S(1)} %deal.1), channel_id=1, replica_groups=mesh['x'=4,'y'=4,'z'=16,'c'=2] {'z'}, dimensions={0} | all-to-all | bytes 8192 | tf_op jit(solution)/shard_map/all_to_all | solution.py:237
  27.9 0.7 copy.6
  28.6 0.0 copy-start.4
  28.6 9.3 %all-to-all-start.1 = ((s32[32,2,16]{2,1,0:T(2,128)}), s32[32,2,16]{2,1,0:T(2,128)S(1)}, u32[]{:S(2)}, u32[]{:S(2)}) async-start(s32[32,2,16]{2,1,0:T(2,128)} %bitcast.2), calls=%async_computation.1 | async-start | bytes 65536 | tf_op jit(solution)/shard_map/all_to_all | solution.py:238
  37.9 0.0 copy-done.4
  37.9 0.0 copy-start.1
  37.9 1.0 copy-done.1
  38.9 0.0 copy-start.2
  38.9 1.0 copy-done.2
  40.0 0.9 own_rows.1
  40.8 4.0 %all-to-all-done.1.wanted_ref = s32[32,2,16]{2,1,0:T(2,128)S(1)} async-done(((s32[32,2,16]{2,1,0:T(2,128)}), s32[32,2,16]{2,1,0:T(2,128)S(1)}, u32[]{:S(2)}, u32[]{:S(2)}) %all-to-all-start.1) | async-done | bytes 4128 | tf_op jit(solution)/shard_map/all_to_all | solution.py:238
  44.9 0.8 serve.1
  45.7 0.0 copy-start.3
  45.7 67.2 %all_to_all.16 = f32[512,4,128]{2,1,0:T(4,128)S(1)} all-to-all(f32[512,4,128]{2,1,0:T(4,128)S(1)} %bitcast.9), channel_id=1, replica_groups=mesh['x'=4,'y'=4,'z'=16,'c'=2] {'z','c','x','y'}, dimensions={0} | all-to-all | bytes 2097152 | tf_op jit(solution)/shard_map/all_to_all | solution.py:243
  112.9 0.0 copy-done.3
  112.9 2.1 %add_up.1 = f32[1024,128]{1,0:T(8,128)} custom-call(s32[8,128]{1,0:T(8,128)S(1)} %get-tuple-element.12.first_ref, s32[8,128]{1,0:T(8,128)S(1)} %get-tuple-element.13.second_ref, f32[2048,128]{1,0:T(8,128)S(1)} %bitcast.10, s32[1024,128]{1,0:T(8,128)S(1)} %copy-done.3), custom_call_target="tpu_custom_call" | custom-call | flops 1073741824 | bytes 2097152 | tf_op jit(solution)/shard_map/add_up/pallas_call | solution.py:212
Async XLA Ops:
  0.0 0.7 copy-start
  28.6 9.3 %copy-start.4 = (s32[1,512,2]{1,2,0:T(2,128)S(1)}, s32[1,512,2]{1,2,0:T(2,128)}, u32[]{:S(2)}) copy-start(s32[1,512,2]{1,2,0:T(2,128)} %param.7) | copy-start | bytes 12292
  28.6 16.3 %all-to-all-start.1 = ((s32[32,2,16]{2,1,0:T(2,128)}), s32[32,2,16]{2,1,0:T(2,128)S(1)}, u32[]{:S(2)}, u32[]{:S(2)}) async-start(s32[32,2,16]{2,1,0:T(2,128)} %bitcast.2), calls=%async_computation.1 | async-start | bytes 65536 | tf_op jit(solution)/shard_map/all_to_all | solution.py:238
  37.9 1.0 copy-start.1
  38.9 1.0 copy-start.2
  45.7 67.2 %copy-start.3 = (s32[1024,128]{1,0:T(8,128)S(1)}, s32[1024,128]{1,0:T(8,128)}, u32[]{:S(2)}) copy-start(s32[1024,128]{1,0:T(8,128)} %orbit_ref.3) | copy-start | bytes 1572868

commit v9 on v8

--- a/solution.py
+++ b/solution.py
@@ -85,8 +85,8 @@
         yield first * width, halves_added(product)
 
 
-def own_kernel(amplitudes_ref, orbit_ref, places_ref, table_ref, own_ref, landing_ref):
-    table_ref[...] = two_parts(amplitudes_ref[...] * orbit_factor(orbit_ref[...]))
+def own_kernel(weighted_ref, places_ref, table_ref, own_ref, landing_ref):
+    table_ref[...] = two_parts(weighted_ref[...])
     slots, total = places_ref.shape
     run = 32
     lanes = landing_ref.shape[1]
@@ -106,8 +106,8 @@
         own_ref[first : first + rows.shape[0], :] = rows
 
 
-def own_rows(amplitudes, orbit, places):
-    blocks, columns = amplitudes.shape
+def own_rows(weighted, places):
+    blocks, columns = weighted.shape
     rows = places.size
     return pl.pallas_call(
         own_kernel,
@@ -116,16 +116,16 @@
             jax.ShapeDtypeStruct((rows, columns), jnp.float32),
             jax.ShapeDtypeStruct((rows // 128, 128), jnp.int32),
         ),
-        in_specs=[IN_VMEM] * 3,
+        in_specs=[IN_VMEM] * 2,
         out_specs=(IN_VMEM,) * 3,
         compiler_params=pltpu.CompilerParams(vmem_limit_bytes=16 * MIB),
         cost_estimate=pl.CostEstimate(
-            flops=4 * rows * blocks * columns,
-            bytes_accessed=20 * blocks * columns,
-            transcendentals=blocks * columns,
+            flops=rows * columns,
+            bytes_accessed=rows * columns,
+            transcendentals=0,
         ),
         name="own_rows",
-    )(amplitudes, orbit, places)
+    )(weighted, places)
 
 
 def serve_kernel(wanted_ref, table_ref, own_ref, out_ref, landing_ref):
@@ -238,7 +238,8 @@
     wanted = lax.all_to_all(
         asked.transpose(2, 1, 0), PLANE, split_axis=0, concat_axis=0, tiled=True
     )
-    table, own, landing = own_rows(amplitudes, orbit_index, targets.reshape(-1, slots).T)
+    weighted = amplitudes * orbit_factor(orbit_index)
+    table, own, landing = own_rows(weighted, targets.reshape(-1, slots).T)
     outgoing, wanted_landing = serve(wanted, table, own)
     arrived = lax.all_to_all(
         outgoing.reshape(nz * plane, 2 * slots, columns),

time: 115 us -> 115 us (level)
  local copies, waits for them, and re-layouts: 3.47 us -> 1.39 us
  other arithmetic: 0 us -> 1.44 us
    unnamed x10 -> x6, local copies, waits for them, and re-layouts: 2.77 us -> 0.7 us
    mul x0 -> x1, other arithmetic: none -> 1.44 us  [per_device(): weighted = amplitudes * orbit_factor(orbit_index)]
  transfers between devices with their start and end apart: 1 -> 1, of which waited for: 1 -> 1; matrix products, arithmetic and copies ran while one was open for 0% -> 1% of each run, Pallas kernels for 1% -> 1%
where the time goes in v9:
time: 115 us
  blocking collectives  94.1 us (82%)
  starting transfers between devices  9.16 us (8%)
  waiting for transfers between devices  4.7 us (4%)
  Pallas kernels  3.96 us (3%)
  other arithmetic  1.44 us (1%)
  local copies, waits for them, and re-layouts  1.39 us (1%)
    all_to_all x1, blocking collectives, per_device(): lax.all_to_all(outgoing.reshape(nz * plane, 2 * slots, columns), PEERS, s...  67.2 us
    all_to_all x1, blocking collectives, per_device(): asked = lax.all_to_all(asked, 'z', split_axis=0, concat_axis=0, tiled=True)  26.9 us
    all_to_all x1, starting transfers between devices, per_device(): lax.all_to_all(asked.transpose(2, 1, 0), PLANE, split_axis=0, concat_axis...  9.16 us
    all_to_all x1, waiting for transfers between devices, per_device(): lax.all_to_all(asked.transpose(2, 1, 0), PLANE, split_axis=0, concat_axis...  4.7 us
  transfers between devices with their start and end apart: 1, of which 1 were waited for; matrix products, arithmetic and copies ran while one was open for 1% of the time, Pallas kernels for 1%

profile of v9, /device:TPU:1, one launch (start us, length us, event | category | flops | bytes accessed | tf_op | source)
XLA Modules:
  0.0 114.9 jit_solution(18318074362623311298)
XLA Ops:
  0.0 0.0 copy-start.2
  0.0 0.7 copy-done.2
  0.7 0.2 deal.1
  0.9 26.9 %all_to_all.15 = s32[16,2,32]{2,1,0:T(2,128)S(1)} all-to-all(s32[16,2,32]{2,1,0:T(2,128)S(1)} %deal.1), channel_id=1, replica_groups=mesh['x'=4,'y'=4,'z'=16,'c'=2] {'z'}, dimensions={0} | all-to-all | bytes 8192 | tf_op jit(solution)/shard_map/all_to_all | solution.py:237
  27.9 0.7 copy.6
  28.6 9.2 %all-to-all-start.1 = ((s32[32,2,16]{2,1,0:T(2,128)}), s32[32,2,16]{2,1,0:T(2,128)S(1)}, u32[]{:S(2)}, u32[]{:S(2)}) async-start(s32[32,2,16]{2,1,0:T(2,128)} %bitcast.2), calls=%async_computation.1 | async-start | bytes 65536 | tf_op jit(solution)/shard_map/all_to_all | solution.py:238
  37.7 0.0 copy-start.1
  37.7 1.4 %sqrt_multiply_fusion.weighted_ref = f32[1024,128]{1,0:T(8,128)S(1)} fusion(f32[1024,128]{1,0:T(8,128)} %param.4, s32[1024,128]{1,0:T(8,128)} %orbit_ref.1), kind=kLoop, calls=%fused_computation | loop fusion | flops 655360 | bytes 1572864 | tf_op jit(solution)/shard_map/mul | solution.py:241
  39.2 0.0 copy-done.1
  39.2 0.8 own_rows.1
  40.0 4.7 %all-to-all-done.1.wanted_ref = s32[32,2,16]{2,1,0:T(2,128)S(1)} async-done(((s32[32,2,16]{2,1,0:T(2,128)}), s32[32,2,16]{2,1,0:T(2,128)S(1)}, u32[]{:S(2)}, u32[]{:S(2)}) %all-to-all-start.1) | async-done | bytes 4128 | tf_op jit(solution)/shard_map/all_to_all | solution.py:238
  44.7 0.8 serve.1
  45.6 0.0 copy-start
  45.6 67.2 %all_to_all.16 = f32[512,4,128]{2,1,0:T(4,128)S(1)} all-to-all(f32[512,4,128]{2,1,0:T(4,128)S(1)} %bitcast.9), channel_id=1, replica_groups=mesh['x'=4,'y'=4,'z'=16,'c'=2] {'z','c','x','y'}, dimensions={0} | all-to-all | bytes 2097152 | tf_op jit(solution)/shard_map/all_to_all | solution.py:244
  112.8 0.0 copy-done
  112.8 2.1 %add_up.1 = f32[1024,128]{1,0:T(8,128)} custom-call(s32[8,128]{1,0:T(8,128)S(1)} %get-tuple-element.12.first_ref, s32[8,128]{1,0:T(8,128)S(1)} %get-tuple-element.13.second_ref, f32[2048,128]{1,0:T(8,128)S(1)} %bitcast.10, s32[1024,128]{1,0:T(8,128)S(1)} %copy-done), custom_call_target="tpu_custom_call" | custom-call | flops 1073741824 | bytes 2097152 | tf_op jit(solution)/shard_map/add_up/pallas_call | solution.py:212
Async XLA Ops:
  0.0 0.7 copy-start.2
  28.6 16.2 %all-to-all-start.1 = ((s32[32,2,16]{2,1,0:T(2,128)}), s32[32,2,16]{2,1,0:T(2,128)S(1)}, u32[]{:S(2)}, u32[]{:S(2)}) async-start(s32[32,2,16]{2,1,0:T(2,128)} %bitcast.2), calls=%async_computation.1 | async-start | bytes 65536 | tf_op jit(solution)/shard_map/all_to_all | solution.py:238
  37.7 1.5 %copy-start.1 = (s32[1,512,2]{1,2,0:T(2,128)S(1)}, s32[1,512,2]{1,2,0:T(2,128)}, u32[]{:S(2)}) copy-start(s32[1,512,2]{1,2,0:T(2,128)} %param.7) | copy-start | bytes 12292
  45.6 67.2 %copy-start = (s32[1024,128]{1,0:T(8,128)S(1)}, s32[1024,128]{1,0:T(8,128)}, u32[]{:S(2)}) copy-start(s32[1024,128]{1,0:T(8,128)} %orbit_ref.1) | copy-start | bytes 1572868

commit v10 on v8

--- a/solution.py
+++ b/solution.py
@@ -141,7 +141,7 @@
     numbers = [square[slot * lines : (slot + 1) * lines, :] for slot in range(slots)]
     turned = [whole[:, slot * lines : (slot + 1) * lines] for slot in range(slots)]
     columns = [turn[:, line : line + 1] for turn in turned for line in range(lines)]
-    for first, rows in picked(columns, table_ref[...], 8):
+    for first, rows in picked(columns, table_ref[...], 16):
         slot, start = divmod(first, peers)
         out_ref[
             pl.ds(start * 2 * slots + slots + slot, rows.shape[0], stride=2 * slots), :

time: 115 us -> 115 us (level)
  no operation moved by 1% of the time
where the time goes in v10:
time: 115 us
  blocking collectives  94.1 us (82%)
  starting transfers between devices  9.3 us (8%)
  waiting for transfers between devices  4.03 us (4%)
  Pallas kernels  3.99 us (3%)
  local copies, waits for them, and re-layouts  3.47 us (3%)
    all_to_all x1, blocking collectives, per_device(): lax.all_to_all(outgoing.reshape(nz * plane, 2 * slots, columns), PEERS, s...  67.2 us
    all_to_all x1, blocking collectives, per_device(): asked = lax.all_to_all(asked, 'z', split_axis=0, concat_axis=0, tiled=True)  26.9 us
    all_to_all x1, starting transfers between devices, per_device(): lax.all_to_all(asked.transpose(2, 1, 0), PLANE, split_axis=0, concat_axis...  9.3 us
    all_to_all x1, waiting for transfers between devices, per_device(): lax.all_to_all(asked.transpose(2, 1, 0), PLANE, split_axis=0, concat_axis...  4.03 us
    unnamed x10, local copies, waits for them, and re-layouts  2.77 us
  transfers between devices with their start and end apart: 1, of which 1 were waited for; matrix products, arithmetic and copies ran while one was open for 0% of the time, Pallas kernels for 1%

profile of v10, /device:TPU:1, one launch (start us, length us, event | category | flops | bytes accessed | tf_op | source)
XLA Modules:
  0.0 115.0 jit_solution(8200605370072764524)
XLA Ops:
  0.0 0.0 copy-start
  0.0 0.7 copy-done
  0.7 0.2 deal.1
  0.9 26.9 %all_to_all.15 = s32[16,2,32]{2,1,0:T(2,128)S(1)} all-to-all(s32[16,2,32]{2,1,0:T(2,128)S(1)} %deal.1), channel_id=1, replica_groups=mesh['x'=4,'y'=4,'z'=16,'c'=2] {'z'}, dimensions={0} | all-to-all | bytes 8192 | tf_op jit(solution)/shard_map/all_to_all | solution.py:237
  27.9 0.7 copy.6
  28.6 0.0 copy-start.4
  28.6 9.3 %all-to-all-start.1 = ((s32[32,2,16]{2,1,0:T(2,128)}), s32[32,2,16]{2,1,0:T(2,128)S(1)}, u32[]{:S(2)}, u32[]{:S(2)}) async-start(s32[32,2,16]{2,1,0:T(2,128)} %bitcast.2), calls=%async_computation.1 | async-start | bytes 65536 | tf_op jit(solution)/shard_map/all_to_all | solution.py:238
  37.9 0.0 copy-done.4
  37.9 0.0 copy-start.1
  37.9 1.0 copy-done.1
  38.9 0.0 copy-start.2
  38.9 1.0 copy-done.2
  40.0 0.9 own_rows.1
  40.8 4.0 %all-to-all-done.1.wanted_ref = s32[32,2,16]{2,1,0:T(2,128)S(1)} async-done(((s32[32,2,16]{2,1,0:T(2,128)}), s32[32,2,16]{2,1,0:T(2,128)S(1)}, u32[]{:S(2)}, u32[]{:S(2)}) %all-to-all-start.1) | async-done | bytes 4128 | tf_op jit(solution)/shard_map/all_to_all | solution.py:238
  44.9 0.8 serve.1
  45.7 0.0 copy-start.3
  45.7 67.2 %all_to_all.16 = f32[512,4,128]{2,1,0:T(4,128)S(1)} all-to-all(f32[512,4,128]{2,1,0:T(4,128)S(1)} %bitcast.9), channel_id=1, replica_groups=mesh['x'=4,'y'=4,'z'=16,'c'=2] {'z','c','x','y'}, dimensions={0} | all-to-all | bytes 2097152 | tf_op jit(solution)/shard_map/all_to_all | solution.py:243
  112.9 0.0 copy-done.3
  112.9 2.1 %add_up.1 = f32[1024,128]{1,0:T(8,128)} custom-call(s32[8,128]{1,0:T(8,128)S(1)} %get-tuple-element.12.first_ref, s32[8,128]{1,0:T(8,128)S(1)} %get-tuple-element.13.second_ref, f32[2048,128]{1,0:T(8,128)S(1)} %bitcast.10, s32[1024,128]{1,0:T(8,128)S(1)} %copy-done.3), custom_call_target="tpu_custom_call" | custom-call | flops 1073741824 | bytes 2097152 | tf_op jit(solution)/shard_map/add_up/pallas_call | solution.py:212
Async XLA Ops:
  0.0 0.7 copy-start
  28.6 9.3 %copy-start.4 = (s32[1,512,2]{1,2,0:T(2,128)S(1)}, s32[1,512,2]{1,2,0:T(2,128)}, u32[]{:S(2)}) copy-start(s32[1,512,2]{1,2,0:T(2,128)} %param.7) | copy-start | bytes 12292
  28.6 16.3 %all-to-all-start.1 = ((s32[32,2,16]{2,1,0:T(2,128)}), s32[32,2,16]{2,1,0:T(2,128)S(1)}, u32[]{:S(2)}, u32[]{:S(2)}) async-start(s32[32,2,16]{2,1,0:T(2,128)} %bitcast.2), calls=%async_computation.1 | async-start | bytes 65536 | tf_op jit(solution)/shard_map/all_to_all | solution.py:238
  37.9 1.0 copy-start.1
  38.9 1.0 copy-start.2
  45.7 67.2 %copy-start.3 = (s32[1024,128]{1,0:T(8,128)S(1)}, s32[1024,128]{1,0:T(8,128)}, u32[]{:S(2)}) copy-start(s32[1024,128]{1,0:T(8,128)} %orbit_ref.3) | copy-start | bytes 1572868
